TPU v7x, 32 devices: a whole 2x2x4 slice. The times are simulated.
32 devices in a mesh: row: 8 (over z, core), col: 4 (over y, x).
Axes of the slice: x: 2, y: 2, z: 4, core: 2. Of those that a mesh axis runs over, the one named last changes fastest.
Arguments:
- matrix: bfloat16 [12288, 12288], P('row', 'col'), may hold values from -8 to 8, as said below
- panels: bfloat16 [2, 12288, 128], P(None, 'row'), may hold values from -1 to 1
Outputs:
- updated: bfloat16 [12288, 12288], P('row', 'col')
Inputs may be any that keep to these rules, and one draw needn't show every extreme that they name: matrix is exactly symmetric.
All inputs are finite; a program needn't handle non-finite values.
Results may differ from a plain program's by a relative error of at most 0.015.
Values may be sent and summed in bfloat16 or wider, within the bound.
No kernel may reach another device: no remote copies, remote signals or barrier semaphores. Data moves between devices by JAX's collectives and lax.ppermute only.
A program may use at most 128 MiB of HBM per device.

v0:
```python
import jax
import jax.numpy as jnp
from jax import lax
from jax.sharding import PartitionSpec as P

PANELS = 2


def spread(block, axis, source):
    block = jnp.where(lax.axis_index(axis) == source, block, jnp.zeros_like(block))
    return lax.psum(block, axis)


def per_device(matrix, panels):
    row_count = lax.axis_size("row")
    col_count = lax.axis_size("col")
    owner_ratio = row_count // col_count
    row_index = lax.axis_index("row")
    col_index = lax.axis_index("col")
    a_tile = matrix
    n_rows = a_tile.shape[0]
    n_cols = a_tile.shape[1]
    for panel in range(PANELS):
        v_rows = panels[panel]
        gathered = lax.all_gather(v_rows, "row", axis=0, tiled=True)
        v_cols = lax.dynamic_slice_in_dim(gathered, col_index * n_cols, n_cols, 0)
        tile_now = a_tile
        av_fine = lax.psum_scatter(
            lax.dot_general(
                tile_now, v_rows, (((0,), (0,)), ((), ())), preferred_element_type=jnp.float32
            ),
            "row",
            scatter_dimension=0,
            tiled=True,
        )
        av_cols = lax.all_gather(av_fine, "row", axis=0, tiled=True)
        own_rows = lax.dynamic_slice_in_dim(av_cols, row_index % owner_ratio * n_rows, n_rows, 0)
        av_rows = spread(own_rows, "col", row_index // owner_ratio)
        local_sum = jnp.dot(v_rows.astype(jnp.float32).T, av_rows, precision=lax.Precision.HIGHEST)
        curvature = lax.psum(local_sum.astype(jnp.bfloat16), "row").astype(jnp.float32)
        w_cols = (
            av_cols
            - 0.5 * jnp.dot(v_cols.astype(jnp.float32), curvature, precision=lax.Precision.HIGHEST)
        ).astype(jnp.bfloat16)
        w_rows = (
            av_rows
            - 0.5 * jnp.dot(v_rows.astype(jnp.float32), curvature, precision=lax.Precision.HIGHEST)
        ).astype(jnp.bfloat16)
        update = lax.dot_general(
            v_rows, w_cols, (((1,), (1,)), ((), ())), preferred_element_type=jnp.float32
        )
        update = update + lax.dot_general(
            w_rows, v_cols, (((1,), (1,)), ((), ())), preferred_element_type=jnp.float32
        )
        a_tile = (a_tile.astype(jnp.float32) - update).astype(jnp.bfloat16)
    return a_tile


def solution(mesh):
    in_specs = (P("row", "col"), P(None, "row", None))
    out_specs = P("row", "col")
    return jax.shard_map(
        per_device, mesh=mesh, in_specs=in_specs, out_specs=out_specs, check_vma=False
    )
```

profile of v0, /device:TPU:0, one launch (start us, length us, event | category | flops | bytes accessed | tf_op | source)
XLA Modules:
  0.0 393.4 jit_solution(9624634092060317979)
XLA Ops:
  6.5 0.0 reduce-scatter.3.cloned.1.call-start
  6.5 7.5 %fusion.34 = f32[3072,128]{1,0:T(8,128)} fusion(bf16[1536,3072]{1,0:T(8,128)(2,1)} %param.2, bf16[2,1536,128]{2,1,0:T(8,128)(2,1)} %param.3), kind=kOutput, calls=%fused_computation.44 | convolution fusion | flops 1207959552 | bytes 11403264 | tf_op jit(solution)/shard_map/dot_general | solution.py:29
  14.1 0.0 reduce-scatter.3.cloned.1.call-update
  14.1 0.0 all-gather.7.cloned.1.call-start
  14.2 37.0 %reduce-scatter.3.cloned.1.call-done = f32[384,128]{1,0:T(8,128)} async-done(((f32[3072,128]{1,0:T(8,128)}), f32[384,128]{1,0:T(8,128)}) %reduce-scatter.3.cloned.1.call-update) | async-done | bytes 196624 | tf_op jit(solution)/shard_map/reduce_scatter | solution.py:28
  51.1 0.0 all-gather.7.cloned.1.call-update
  51.2 0.0 all-reduce.3.cloned.1.call-start
  51.2 25.2 %all-gather.7.cloned.1.call-done = f32[3072,128]{1,0:T(8,128)} async-done(((f32[384,128]{1,0:T(8,128)}), f32[3072,128]{1,0:T(8,128)}) %all-gather.7.cloned.1.call-update) | async-done | bytes 1572880 | tf_op jit(solution)/shard_map/all_gather | solution.py:36
  76.4 2.1 dynamic-slice_select_fusion.1
  78.5 0.0 all-reduce.3.cloned.1.call-update
  78.5 0.0 all-gather.11.cloned.1.call-start
  78.5 0.0 copy-done
  78.5 0.9 fusion.48
  79.5 0.0 all-gather.11.cloned.1.call-update
  79.5 0.0 reduce-scatter.5.cloned.1.call-start
  79.5 0.0 copy-start.1
  79.6 12.8 %copy.3 = bf16[1536,3072]{0,1:T(8,128)(2,1)} copy(bf16[1536,3072]{1,0:T(8,128)(2,1)} %param.2) | data formatting | bytes 18874368 | tf_op args[0]
  92.3 34.9 %all-reduce.3.cloned.1.call-done = f32[1536,128]{1,0:T(8,128)} async-done(((f32[1536,128]{1,0:T(8,128)}), f32[1536,128]{1,0:T(8,128)}) %all-reduce.3.cloned.1.call-update) | async-done | bytes 786448 | tf_op jit(solution)/shard_map/psum | solution.py:11
  127.3 1.9 fusion.14
  129.2 29.9 %psum.29 = bf16[128,128]{0,1:T(8,128)(2,1)S(1)} all-reduce(bf16[128,128]{0,1:T(8,128)(2,1)S(1)} %fusion.14), channel_id=1, replica_groups=mesh['row'=8,'col'=4] {'row'}, use_global_device_ids=true, to_apply=%region_2.3 | all-reduce | flops 16384 | bytes 65536 | tf_op jit(solution)/shard_map/psum | solution.py:40
  159.1 8.3 %all-gather.11.cloned.1.call-done = bf16[1,12288,128]{2,1,0:T(8,128)(2,1)} async-done(((bf16[1,1536,128]{2,1,0:T(8,128)(2,1)}), bf16[1,12288,128]{2,1,0:T(8,128)(2,1)}) %all-gather.11.cloned.1.call-update) | async-done | bytes 3145744 | tf_op jit(solution)/shard_map/all_gather | solution.py:25
  167.4 0.0 copy-done.1
  167.4 1.5 fusion.6
  168.9 0.0 copy-start.2
  168.9 8.0 %fusion.30 = f32[3072,1536]{1,0:T(8,128)} fusion(bf16[3072,128]{1,0:T(8,128)(2,1)S(1)} %fusion.6, bf16[2,1536,128]{2,1,0:T(8,128)(2,1)S(1)} %copy-done), kind=kOutput, calls=%fused_computation.40 | convolution fusion | flops 1207959552 | bytes 20054016 | tf_op jit(solution)/shard_map/dot_general | solution.py:49
  176.9 0.3 fusion.13
  177.2 14.6 %fusion.3 = bf16[1536,3072]{0,1:T(8,128)(2,1)} fusion(f32[3072,1536]{1,0:T(8,128)} %fusion.30, bf16[1536,3072]{0,1:T(8,128)(2,1)} %copy.3, bf16[1536,128]{1,0:T(8,128)(2,1)S(1)} %fusion.13, bf16[1,12288,128]{2,1,0:T(8,128)(2,1)} %all-gather.11.cloned.1.call-done, s32[]{:T(128)S(6)} %select_n.34), kind=kOutput, calls=%fused_computation.5 | convolution fusion | flops 1226833920 | bytes 38928388 | tf_op jit(solution)/shard_map/dot_general | solution.py:52
  191.8 7.5 %fusion.28 = f32[3072,128]{1,0:T(8,128)} fusion(bf16[1536,3072]{0,1:T(8,128)(2,1)} %fusion.3, bf16[2,1536,128]{2,1,0:T(8,128)(2,1)S(1)} %copy-done), kind=kOutput, calls=%fused_computation.38 | convolution fusion | flops 1207959552 | bytes 11403264 | tf_op jit(solution)/shard_map/dot_general | solution.py:29
  199.2 0.0 reduce-scatter.5.cloned.1.call-update
  199.2 0.0 all-gather.9.cloned.1.call-start
  199.3 33.1 %reduce-scatter.5.cloned.1.call-done = f32[384,128]{1,0:T(8,128)} async-done(((f32[3072,128]{1,0:T(8,128)}), f32[384,128]{1,0:T(8,128)}) %reduce-scatter.5.cloned.1.call-update) | async-done | bytes 196624 | tf_op jit(solution)/shard_map/reduce_scatter | solution.py:28
  232.4 0.0 all-gather.9.cloned.1.call-update
  232.5 0.0 all-reduce.5.cloned.1.call-start
  232.5 25.2 %all-gather.9.cloned.1.call-done = f32[3072,128]{1,0:T(8,128)} async-done(((f32[384,128]{1,0:T(8,128)}), f32[3072,128]{1,0:T(8,128)}) %all-gather.9.cloned.1.call-update) | async-done | bytes 1572880 | tf_op jit(solution)/shard_map/all_gather | solution.py:36
  257.7 2.1 dynamic-slice_select_fusion
  259.8 0.0 all-reduce.5.cloned.1.call-update
  259.8 0.0 all-gather.13.cloned.1.call-start
  259.9 0.7 all-gather.13.cloned.1.call-update
  260.6 48.0 %all-reduce.5.cloned.1.call-done = f32[1536,128]{1,0:T(8,128)} async-done(((f32[1536,128]{1,0:T(8,128)}), f32[1536,128]{1,0:T(8,128)}) %all-reduce.5.cloned.1.call-update) | async-done | bytes 786448 | tf_op jit(solution)/shard_map/psum | solution.py:11
  308.6 1.9 fusion.15
  310.5 30.2 %psum.31 = bf16[128,128]{0,1:T(8,128)(2,1)S(1)} all-reduce(bf16[128,128]{0,1:T(8,128)(2,1)S(1)} %fusion.15), channel_id=1, replica_groups=mesh['row'=8,'col'=4] {'row'}, use_global_device_ids=true, to_apply=%region_5.6 | all-reduce | flops 16384 | bytes 65536 | tf_op jit(solution)/shard_map/psum | solution.py:40
  340.7 8.1 %all-gather.13.cloned.1.call-done = bf16[1,12288,128]{2,1,0:T(8,128)(2,1)} async-done(((bf16[1,1536,128]{2,1,0:T(8,128)(2,1)}), bf16[1,12288,128]{2,1,0:T(8,128)(2,1)}) %all-gather.13.cloned.1.call-update) | async-done | bytes 3145744 | tf_op jit(solution)/shard_map/all_gather | solution.py:25
  348.8 2.0 fusion.7
  350.9 0.0 copy-start.3
  350.9 8.0 %fusion.24 = f32[3072,1536]{1,0:T(8,128)} fusion(bf16[3072,128]{1,0:T(8,128)(2,1)S(1)} %fusion.7, bf16[2,1536,128]{2,1,0:T(8,128)(2,1)S(1)} %copy-done), kind=kOutput, calls=%fused_computation.34 | convolution fusion | flops 1207959552 | bytes 20054016 | tf_op jit(solution)/shard_map/dot_general | solution.py:49
  358.9 0.3 fusion.12
  359.1 14.8 %fusion.1 = bf16[1536,3072]{0,1:T(8,128)(2,1)} fusion(f32[3072,1536]{1,0:T(8,128)} %fusion.24, bf16[1536,3072]{0,1:T(8,128)(2,1)} %fusion.3, bf16[1536,128]{1,0:T(8,128)(2,1)S(1)} %fusion.12, bf16[1,12288,128]{2,1,0:T(8,128)(2,1)} %all-gather.13.cloned.1.call-done, s32[]{:T(128)S(6)} %select_n.34), kind=kOutput, calls=%fused_computation.2 | convolution fusion | flops 1226833920 | bytes 38928388 | tf_op jit(solution)/shard_map/dot_general | solution.py:52
  374.0 12.6 %copy.6 = bf16[1536,3072]{1,0:T(8,128)(2,1)} copy(bf16[1536,3072]{0,1:T(8,128)(2,1)} %fusion.1) | data formatting | bytes 18874368 | tf_op jit(solution)/shard_map/convert_element_type | solution.py:55
  (3 shorter events, 0.0 us)
Async XLA Ops:
  6.5 72.0 %copy-start = (bf16[2,1536,128]{2,1,0:T(8,128)(2,1)S(1)}, bf16[2,1536,128]{2,1,0:T(8,128)(2,1)}, u32[]{:S(2)}) copy-start(bf16[2,1536,128]{2,1,0:T(8,128)(2,1)} %param.3) | copy-start | bytes 2359300
  6.5 44.6 %reduce-scatter.3.cloned.1.call-start = ((), (), s32[]{:S(2)}) async-start(), calls=%async_computation.2 | async-start | bytes 1769472 | tf_op jit(solution)/shard_map/reduce_scatter | solution.py:28
  14.1 62.3 %all-gather.7.cloned.1.call-start = ((), (), s32[]{:S(2)}) async-start(), calls=%async_computation.3 | async-start | bytes 1769472 | tf_op jit(solution)/shard_map/all_gather | solution.py:36
  51.2 76.1 %all-reduce.3.cloned.1.call-start = ((), (), s32[]{:S(2)}) async-start(), calls=%async_computation.4 | async-start | bytes 1572864 | tf_op jit(solution)/shard_map/psum | solution.py:11
  78.5 88.9 %all-gather.11.cloned.1.call-start = ((), (), s32[]{:S(2)}) async-start(), calls=%async_computation.8 | async-start | bytes 3538944 | tf_op jit(solution)/shard_map/all_gather | solution.py:25
  79.5 152.9 %reduce-scatter.5.cloned.1.call-start = ((), (), s32[]{:S(2)}) async-start(), calls=%async_computation.5 | async-start | bytes 1769472 | tf_op jit(solution)/shard_map/reduce_scatter | solution.py:28
  79.5 87.9 %copy-start.1 = (f32[3072,128]{1,0:T(8,128)S(1)}, f32[3072,128]{1,0:T(8,128)}, u32[]{:S(2)}) copy-start(f32[3072,128]{1,0:T(8,128)} %all-gather.7.cloned.1.call-done) | copy-start | bytes 4718596
  168.9 8.0 %copy-start.2 = (f32[1536,128]{1,0:T(8,128)S(1)}, f32[1536,128]{1,0:T(8,128)}, u32[]{:S(2)}) copy-start(f32[1536,128]{1,0:T(8,128)} %all-reduce.3.cloned.1.call-done) | copy-start | bytes 2359300
  199.2 58.5 %all-gather.9.cloned.1.call-start = ((), (), s32[]{:S(2)}) async-start(), calls=%async_computation.6 | async-start | bytes 1769472 | tf_op jit(solution)/shard_map/all_gather | solution.py:36
  232.5 76.1 %all-reduce.5.cloned.1.call-start = ((), (), s32[]{:S(2)}) async-start(), calls=%async_computation.7 | async-start | bytes 1572864 | tf_op jit(solution)/shard_map/psum | solution.py:11
  259.8 89.0 %all-gather.13.cloned.1.call-start = ((), (), s32[]{:S(2)}) async-start(), calls=%async_computation.9 | async-start | bytes 3538944 | tf_op jit(solution)/shard_map/all_gather | solution.py:25
  350.9 8.0 %copy-start.3 = (f32[1536,128]{1,0:T(8,128)S(1)}, f32[1536,128]{1,0:T(8,128)}, u32[]{:S(2)}) copy-start(f32[1536,128]{1,0:T(8,128)} %all-reduce.5.cloned.1.call-done) | copy-start | bytes 2359300
Sparse Core Ops, SparseCore 0:
  14.2 36.8 reduce-scatter.2
  52.8 23.5 all-gather.6
  79.5 47.7 all-reduce.2
  128.8 38.5 all-gather.10
  199.4 33.0 reduce-scatter.4
  233.9 23.7 all-gather.8
  260.7 47.7 all-reduce.4
  310.2 38.6 all-gather.12
where the time goes:
time: 394 us; the launch traced here: 393 us
  waiting for transfers between devices  221 us (56%)
  matrix products  68.3 us (17%)
  blocking collectives  60.1 us (15%)
  local copies, waits for them, and re-layouts  26.3 us (7%)
  between operations  13.6 us (3%)
  other arithmetic  4.14 us (1%)
    psum x2, waiting for transfers between devices, spread(): return lax.psum(block, axis)  82.9 us
    reduce_scatter x2, waiting for transfers between devices, per_device(): lax.psum_scatter(lax.dot_general(tile_now, v_rows, (((0,), (0,)), ((), ()...  70.1 us
    psum x2, blocking collectives, per_device(): lax.psum(local_sum.astype(jnp.bfloat16), 'row').astype(jnp.float32)  60.1 us
    all_gather x2, waiting for transfers between devices, per_device(): av_cols = lax.all_gather(av_fine, 'row', axis=0, tiled=True)  50.3 us
    dot_general x2, matrix products, per_device(): lax.dot_general(w_rows, v_cols, (((1,), (1,)), ((), ())), preferred_eleme...  29.4 us
    all_gather x2, waiting for transfers between devices, per_device(): gathered = lax.all_gather(v_rows, 'row', axis=0, tiled=True)  16.4 us
    dot_general x2, matrix products, per_device(): lax.dot_general(v_rows, w_cols, (((1,), (1,)), ((), ())), preferred_eleme...  16 us
    dot_general x2, matrix products, per_device(): lax.dot_general(tile_now, v_rows, (((0,), (0,)), ((), ())), preferred_ele...  15 us
  transfers between devices with their start and end apart: 8, of which 8 were waited for; matrix products, arithmetic and copies ran while one was open for 4% of the time, Pallas kernels for 0%

commit v1 on v0

v1 whole, which is shorter than its diff:
```python
import jax
import jax.numpy as jnp
from jax import lax
from jax.sharding import PartitionSpec as P

F32 = jnp.float32
BF16 = jnp.bfloat16


def dot(a, b, ca, cb):
    return lax.dot_general(a, b, (((ca,), (cb,)), ((), ())), preferred_element_type=F32)


def exact(a, b, ca=1, cb=0):
    return lax.dot_general(
        a, b, (((ca,), (cb,)), ((), ())), precision=lax.Precision.HIGHEST, preferred_element_type=F32
    )


def per_device(a_tile, panels):
    rows = lax.axis_size("row")
    cols = lax.axis_size("col")
    ratio = rows // cols
    row = lax.axis_index("row")
    col = lax.axis_index("col")
    group = row // ratio
    member = row % ratio
    n_panels, n_rows, b = panels.shape
    part = n_rows // cols
    width = n_panels * b

    def index(g, m, c):
        return (g * ratio + m) * cols + c

    def spread_pairs(t):
        return [
            (index(g, m, c), index((t - c) % cols, m, g))
            for g in range(cols)
            for m in range(ratio)
            for c in range(cols)
        ]

    def column_blocks(piece):
        pieces = [lax.ppermute(piece, ("row", "col"), spread_pairs(t)) for t in range(cols)]
        block = jnp.zeros((n_rows, width), BF16)
        for t, got in enumerate(pieces):
            block = lax.dynamic_update_slice_in_dim(block, got, (t - group) % cols * part, 0)
        full = jnp.zeros((ratio * n_rows, width), BF16)
        full = lax.dynamic_update_slice_in_dim(full, block, member * n_rows, 0)
        for o in range(1, ratio):
            pairs = [(g * ratio + m, g * ratio + (m + o) % ratio) for g in range(cols) for m in range(ratio)]
            got = lax.ppermute(block, "row", pairs)
            full = lax.dynamic_update_slice_in_dim(full, got, (member - o) % ratio * n_rows, 0)
        return full

    def shift(o):
        return [(c, (c + o) % cols) for c in range(cols)]

    def col_sum(x, wire):
        sent = x.astype(wire)
        total = x
        for o in range(1, cols):
            total = total + lax.ppermute(sent, "col", shift(o)).astype(F32)
        return total

    v_rows = jnp.concatenate([panels[p] for p in range(n_panels)], axis=1)
    v_piece = lax.dynamic_slice_in_dim(v_rows, col * part, part, 0)
    v_cols = column_blocks(v_piece)

    partial = dot(a_tile, v_cols, 1, 0)
    mine = lax.dynamic_slice_in_dim(partial, col * part, part, 0)
    sent = partial.astype(BF16)
    for o in range(1, cols):
        theirs = lax.dynamic_slice_in_dim(sent, (col + o) % cols * part, part, 0)
        mine = mine + lax.ppermute(theirs, "col", shift(o)).astype(F32)
    p_piece = mine.astype(BF16)

    s = col_sum(dot(v_cols[:, :b], v_cols[:, b:], 0, 0), F32)

    p_cols = column_blocks(p_piece)
    p_rows = jnp.zeros((n_rows, width), BF16)
    p_rows = lax.dynamic_update_slice_in_dim(p_rows, p_piece, col * part, 0)
    for o in range(1, cols):
        got = lax.ppermute(p_piece, "col", shift(o))
        p_rows = lax.dynamic_update_slice_in_dim(p_rows, got, (col - o) % cols * part, 0)

    g = col_sum(dot(v_cols, p_cols, 0, 0), BF16)
    c1 = g[:b, :b]
    g12 = g[:b, b:]
    g22 = g[b:, b:]
    k12 = exact(c1, s) - g12
    cross = exact(s, g12, 0, 0)
    c2 = g22 - cross - cross.T + exact(s, exact(c1, s), 0, 0)

    v1 = v_rows[:, :b]
    v2 = v_rows[:, b:]
    x1 = (v1.astype(F32) - exact(v2.astype(F32), s, 1, 1)).astype(BF16)
    mix = jnp.concatenate(
        [
            jnp.concatenate([-c1, k12], axis=1),
            jnp.concatenate([k12.T, -c2], axis=1),
        ],
        axis=0,
    )
    y = exact(v_rows.astype(F32), mix) + p_rows.astype(F32)
    y = y - jnp.concatenate(
        [jnp.zeros((n_rows, b), F32), exact(p_rows[:, :b].astype(F32), s)], axis=1
    )
    left = jnp.concatenate([x1, v2, y.astype(BF16)], axis=1)
    right = jnp.concatenate([p_cols, v_cols], axis=1)
    update = dot(left, right, 1, 1)
    return (a_tile.astype(F32) - update).astype(BF16)


def solution(mesh):
    in_specs = (P("row", "col"), P(None, "row", None))
    out_specs = P("row", "col")
    return jax.shard_map(
        per_device, mesh=mesh, in_specs=in_specs, out_specs=out_specs, check_vma=False
    )
```

time: 394 us -> 136 us (0.35)
  waiting for transfers between devices: 221 us -> 29.3 us
  blocking collectives: 60.1 us -> 0 us
  starting transfers between devices: 0.29 us -> 58.4 us
  matrix products: 68.3 us -> 27 us
  between operations: 13.6 us -> 0.49 us
  local copies, waits for them, and re-layouts: 26.3 us -> 18.5 us
    psum x2 -> x0, waiting for transfers between devices: 82.9 us -> none  [spread(): return lax.psum(block, axis)]
    reduce_scatter x2 -> x0, waiting for transfers between devices: 70.1 us -> none  [per_device(): lax.psum_scatter(lax.dot_general(tile_now, v_rows, (((0,), (0,)), ((), ()...]
    all_gather x4 -> x0, waiting for transfers between devices: 66.8 us -> none  [the longest x2 50.3 us: per_device(): av_cols = lax.all_gather(av_fine, 'row', axis=0, tiled=True)]
    psum x2 -> x0, blocking collectives: 60.1 us -> none  [per_device(): lax.psum(local_sum.astype(jnp.bfloat16), 'row').astype(jnp.float32)]
    ppermute x0 -> x22, starting transfers between devices: none -> 58.4 us  [the longest x8 28 us: column_blocks(): lax.ppermute(piece, ('row', 'col'), spread_pairs(t))]
    dot_general x12 -> x10, matrix products: 68.3 us -> 27 us  [the longest x4 16.1 us: dot(): lax.dot_general(a, b, (((ca,), (cb,)), ((), ())), preferred_element_type=...]
    ppermute x0 -> x22, waiting for transfers between devices: none -> 29.3 us  [the longest x3 12.3 us: per_device(): got = lax.ppermute(p_piece, 'col', shift(o))]
    unnamed x9 -> x12, local copies, waits for them, and re-layouts: 12.8 us -> 0.02 us
  transfers between devices with their start and end apart: 8 -> 22, of which waited for: 8 -> 8; matrix products, arithmetic and copies ran while one was open for 4% -> 11% of each run, Pallas kernels for 0% -> 0%
where the time goes in v1:
time: 136 us; the launch traced here: 135 us
  starting transfers between devices  58.4 us (43%)
  waiting for transfers between devices  29.3 us (22%)
  matrix products  27 us (20%)
  local copies, waits for them, and re-layouts  18.5 us (14%)
  other arithmetic  1.62 us (1%)
    ppermute x8, starting transfers between devices, column_blocks(): lax.ppermute(piece, ('row', 'col'), spread_pairs(t))  28 us
    dot_general x4, matrix products, dot(): lax.dot_general(a, b, (((ca,), (cb,)), ((), ())), preferred_element_type=...  16.1 us
    ppermute x3, starting transfers between devices, per_device(): mine = mine + lax.ppermute(theirs, 'col', shift(o)).astype(F32)  13.5 us
    ppermute x3, waiting for transfers between devices, per_device(): got = lax.ppermute(p_piece, 'col', shift(o))  12.3 us
    dot_general x6, matrix products, exact(): lax.dot_general(a, b, (((ca,), (cb,)), ((), ())), precision=lax.Precision...  10.9 us
    ppermute x3, starting transfers between devices, per_device(): got = lax.ppermute(p_piece, 'col', shift(o))  9.15 us
    ppermute x8, waiting for transfers between devices, column_blocks(): lax.ppermute(piece, ('row', 'col'), spread_pairs(t))  7.9 us
    ppermute x6, starting transfers between devices, col_sum(): total = total + lax.ppermute(sent, 'col', shift(o)).astype(F32)  7.68 us
  transfers between devices with their start and end apart: 22, of which 8 were waited for; matrix products, arithmetic and copies ran while one was open for 11% of the time, Pallas kernels for 0%

profile of v1, /device:TPU:0, one launch (start us, length us, event | category | flops | bytes accessed | tf_op | source)
XLA Modules:
  0.0 135.2 jit_solution(8283634595064856272)
XLA Ops:
  0.0 1.2 slice_bitcast_fusion
  1.2 6.0 %collective-permute-start.2 = (bf16[384,256]{1,0:T(8,128)(2,1)S(1)}, bf16[384,256]{1,0:T(8,128)(2,1)S(1)}, u32[]{:S(2)}, u32[]{:S(2)}) collective-permute-start(bf16[384,256]{1,0:T(8,128)(2,1)S(1)} %fusion.26), channel_id=1, source_target_pairs={{0,16},{1,8},{2,0},{3,24},{4,20},{5,12},{6,4},{7,28},{8,17},{9,9},... | collective-permute-start | bytes 589832 | tf_op jit(solution)/shard_map/ppermute | solution.py:44
  7.2 0.7 collective-permute-start
  7.9 3.2 %collective-permute-start.1 = (bf16[384,256]{1,0:T(8,128)(2,1)S(1)}, bf16[384,256]{1,0:T(8,128)(2,1)S(1)}, u32[]{:S(2)}, u32[]{:S(2)}) collective-permute-start(bf16[384,256]{1,0:T(8,128)(2,1)S(1)} %fusion.26), channel_id=1, source_target_pairs={{0,8},{1,0},{2,24},{3,16},{4,12},{5,4},{6,28},{7,20},{8,9},{9,1},{... | collective-permute-start | bytes 589832 | tf_op jit(solution)/shard_map/ppermute | solution.py:44
  11.1 4.8 %collective-permute-start.3 = (bf16[384,256]{1,0:T(8,128)(2,1)S(1)}, bf16[384,256]{1,0:T(8,128)(2,1)S(1)}, u32[]{:S(2)}, u32[]{:S(2)}) collective-permute-start(bf16[384,256]{1,0:T(8,128)(2,1)S(1)} %fusion.26), channel_id=1, source_target_pairs={{0,24},{1,16},{2,8},{3,0},{4,28},{5,20},{6,12},{7,4},{8,25},{9,17}... | collective-permute-start | bytes 589832 | tf_op jit(solution)/shard_map/ppermute | solution.py:44
  16.3 2.0 %collective-permute-done.1 = bf16[384,256]{1,0:T(8,128)(2,1)S(1)} collective-permute-done((bf16[384,256]{1,0:T(8,128)(2,1)S(1)}, bf16[384,256]{1,0:T(8,128)(2,1)S(1)}, u32[]{:S(2)}, u32[]{:S(2)}) %collective-permute-start.1) | collective-permute-done | bytes 196640 | tf_op jit(solution)/shard_map/ppermute | solution.py:44
  18.6 1.3 collective-permute-done.3
  20.3 0.9 copy.11
  21.5 0.9 collective-permute-done.4
  22.5 5.2 %fusion.38 = (bf16[256,1536]{1,0:T(8,128)(2,1)S(1)}, f32[256,1536]{1,0:T(8,128)S(1)}) fusion(bf16[3072,256]{0,1:T(8,128)(2,1)S(1)} %constant_dynamic-update-slice_fusion.10, bf16[1536,3072]{1,0:T(8,128)(2,1)} %param.2), kind=kOutput, calls=%fused_computation.70 | convolution fusion | flops 2416312320 | bytes 13369344 | tf_op jit(solution)/shard_map/dot_general | solution.py:11
  27.8 9.0 %collective-permute-start.8 = (bf16[384,256]{0,1:T(8,128)(2,1)S(1)}, bf16[384,256]{0,1:T(8,128)(2,1)S(1)}, u32[]{:S(2)}, u32[]{:S(2)}) collective-permute-start(bf16[384,256]{0,1:T(8,128)(2,1)S(1)} %get-tuple-element.7), channel_id=1, source_target_pairs={{0,1},{1,2},{2,3},{3,0},{4,5},{5,6},{6,7},{7,4},{8,9},{9,10},{10,1... | collective-permute-start | bytes 589832 | tf_op jit(solution)/shard_map/ppermute | solution.py:75
  36.8 4.5 %collective-permute-start.9 = (bf16[384,256]{0,1:T(8,128)(2,1)S(1)}, bf16[384,256]{0,1:T(8,128)(2,1)S(1)}, u32[]{:S(2)}, u32[]{:S(2)}) collective-permute-start(bf16[384,256]{0,1:T(8,128)(2,1)S(1)} %get-tuple-element.9), channel_id=1, source_target_pairs={{0,2},{1,3},{2,0},{3,1},{4,6},{5,7},{6,4},{7,5},{8,10},{9,11},{10,... | collective-permute-start | bytes 589832 | tf_op jit(solution)/shard_map/ppermute | solution.py:75
  42.4 2.8 %collective-permute-start.5 = (f32[128,128]{1,0:T(8,128)S(1)}, f32[128,128]{1,0:T(8,128)S(1)}, u32[]{:S(2)}, u32[]{:S(2)}) collective-permute-start(f32[128,128]{1,0:T(8,128)S(1)} %fusion.11), channel_id=1, source_target_pairs={{0,1},{1,2},{2,3},{3,0},{4,5},{5,6},{6,7},{7,4},{8,9},{9,10},{10,1... | collective-permute-start | bytes 196616 | tf_op jit(solution)/shard_map/ppermute | solution.py:63
  45.2 4.7 %collective-permute-done.10 = bf16[384,256]{0,1:T(8,128)(2,1)S(1)} collective-permute-done((bf16[384,256]{0,1:T(8,128)(2,1)S(1)}, bf16[384,256]{0,1:T(8,128)(2,1)S(1)}, u32[]{:S(2)}, u32[]{:S(2)}) %collective-permute-start.10) | collective-permute-done | bytes 196640 | tf_op jit(solution)/shard_map/ppermute | solution.py:75
  49.8 1.0 broadcast.22.clone.1
  50.8 0.8 constant_dynamic-update-slice_fusion.3
  51.7 0.8 collective-permute-start.11
  52.5 4.8 %collective-permute-start.20 = (bf16[384,256]{0,1:T(8,128)(2,1)S(1)}, bf16[384,256]{0,1:T(8,128)(2,1)S(1)}, u32[]{:S(2)}, u32[]{:S(2)}) collective-permute-start(bf16[384,256]{0,1:T(8,128)(2,1)S(1)} %get-tuple-element.6), channel_id=1, source_target_pairs={{0,2},{1,3},{2,0},{3,1},{4,6},{5,7},{6,4},{7,5},{8,10},{9,11},{10,... | collective-permute-start | bytes 589832 | tf_op jit(solution)/shard_map/ppermute | solution.py:84
  57.3 2.6 %collective-permute-start.19 = (bf16[384,256]{0,1:T(8,128)(2,1)S(1)}, bf16[384,256]{0,1:T(8,128)(2,1)S(1)}, u32[]{:S(2)}, u32[]{:S(2)}) collective-permute-start(bf16[384,256]{0,1:T(8,128)(2,1)S(1)} %get-tuple-element.6), channel_id=1, source_target_pairs={{0,1},{1,2},{2,3},{3,0},{4,5},{5,6},{6,7},{7,4},{8,9},{9,10},{10,1... | collective-permute-start | bytes 589832 | tf_op jit(solution)/shard_map/ppermute | solution.py:84
  59.9 2.9 %collective-permute-start.14 = (bf16[384,256]{0,1:T(8,128)(2,1)S(1)}, bf16[384,256]{0,1:T(8,128)(2,1)S(1)}, u32[]{:S(2)}, u32[]{:S(2)}) collective-permute-start(bf16[384,256]{0,1:T(8,128)(2,1)S(1)} %get-tuple-element.6), channel_id=1, source_target_pairs={{0,24},{1,16},{2,8},{3,0},{4,28},{5,20},{6,12},{7,4},{8,25},{9,17}... | collective-permute-start | bytes 589832 | tf_op jit(solution)/shard_map/ppermute | solution.py:44
  62.8 9.7 %collective-permute-start.13 = (bf16[384,256]{0,1:T(8,128)(2,1)S(1)}, bf16[384,256]{0,1:T(8,128)(2,1)S(1)}, u32[]{:S(2)}, u32[]{:S(2)}) collective-permute-start(bf16[384,256]{0,1:T(8,128)(2,1)S(1)} %get-tuple-element.6), channel_id=1, source_target_pairs={{0,16},{1,8},{2,0},{3,24},{4,20},{5,12},{6,4},{7,28},{8,17},{9,9},... | collective-permute-start | bytes 589832 | tf_op jit(solution)/shard_map/ppermute | solution.py:44
  72.5 0.9 broadcast.22
  73.4 0.7 constant_dynamic-update-slice_fusion.9
  74.1 0.7 constant_dynamic-update-slice_fusion.8
  74.8 4.6 %collective-permute-done.13 = bf16[384,256]{0,1:T(8,128)(2,1)S(1)} collective-permute-done((bf16[384,256]{0,1:T(8,128)(2,1)S(1)}, bf16[384,256]{0,1:T(8,128)(2,1)S(1)}, u32[]{:S(2)}, u32[]{:S(2)}) %collective-permute-start.13) | collective-permute-done | bytes 196640 | tf_op jit(solution)/shard_map/ppermute | solution.py:44
  79.4 0.7 constant_dynamic-update-slice_fusion.7
  80.1 0.7 constant_dynamic-update-slice_fusion.6
  81.3 0.9 copy.10
  82.3 1.8 %collective-permute-start.21 = (bf16[384,256]{0,1:T(8,128)(2,1)S(1)}, bf16[384,256]{0,1:T(8,128)(2,1)S(1)}, u32[]{:S(2)}, u32[]{:S(2)}) collective-permute-start(bf16[384,256]{0,1:T(8,128)(2,1)S(1)} %get-tuple-element.6), channel_id=1, source_target_pairs={{0,3},{1,0},{2,1},{3,2},{4,7},{5,4},{6,5},{7,6},{8,11},{9,8},{10,9... | collective-permute-start | bytes 589832 | tf_op jit(solution)/shard_map/ppermute | solution.py:84
  84.0 0.7 constant_dynamic-update-slice_fusion.2
  84.8 0.8 constant_dynamic-update-slice_fusion.1
  85.5 12.3 %collective-permute-done.21 = bf16[384,256]{0,1:T(8,128)(2,1)S(1)} collective-permute-done((bf16[384,256]{0,1:T(8,128)(2,1)S(1)}, bf16[384,256]{0,1:T(8,128)(2,1)S(1)}, u32[]{:S(2)}, u32[]{:S(2)}) %collective-permute-start.21) | collective-permute-done | bytes 196640 | tf_op jit(solution)/shard_map/ppermute | solution.py:84
  97.8 0.7 constant_dynamic-update-slice_fusion
  98.7 1.2 constant_dynamic-update-slice_fusion.5
  99.9 1.2 constant_dynamic-update-slice_fusion.4
  101.9 4.1 %collective-permute-start.17 = (bf16[256,256]{0,1:T(8,128)(2,1)S(1)}, bf16[256,256]{0,1:T(8,128)(2,1)S(1)}, u32[]{:S(2)}, u32[]{:S(2)}) collective-permute-start(bf16[256,256]{0,1:T(8,128)(2,1)S(1)} %get-tuple-element.17), channel_id=1, source_target_pairs={{0,2},{1,3},{2,0},{3,1},{4,6},{5,7},{6,4},{7,5},{8,10},{9,11},{10,... | collective-permute-start | bytes 393224 | tf_op jit(solution)/shard_map/ppermute | solution.py:63
  106.0 2.4 %fusion.14 = f32[1536,128]{0,1:T(8,128)} fusion(f32[128,128]{1,0:T(8,128)S(1)} %copy-done.1, bf16[1536,256]{0,1:T(8,128)(2,1)} %constant_dynamic-update-slice_fusion), kind=kOutput, calls=%fused_computation.20 | convolution fusion | flops 301989888 | bytes 1245184 | tf_op jit(solution)/shard_map/dot_general | solution.py:15
  108.4 2.6 %collective-permute-done.17 = bf16[256,256]{0,1:T(8,128)(2,1)S(1)} collective-permute-done((bf16[256,256]{0,1:T(8,128)(2,1)S(1)}, bf16[256,256]{0,1:T(8,128)(2,1)S(1)}, u32[]{:S(2)}, u32[]{:S(2)}) %collective-permute-start.17) | collective-permute-done | bytes 131104 | tf_op jit(solution)/shard_map/ppermute | solution.py:63
  111.0 0.8 collective-permute-done.16
  111.8 0.8 convert_add_fusion
  112.6 1.7 %fusion.32 = f32[128,128]{1,0:T(8,128)} fusion(f32[128,128]{1,0:T(8,128)S(1)} %copy-done.1, f32[256,256]{0,1:T(8,128)} %convert_add_fusion), kind=kOutput, calls=%fused_computation.48 | convolution fusion | flops 25165824 | bytes 196608 | tf_op jit(solution)/shard_map/dot_general | solution.py:15
  114.3 1.7 %fusion.30 = f32[128,128]{1,0:T(8,128)} fusion(f32[128,128]{1,0:T(8,128)S(1)} %copy-done.1, f32[256,256]{0,1:T(8,128)} %convert_add_fusion), kind=kOutput, calls=%fused_computation.45 | convolution fusion | flops 25165824 | bytes 196608 | tf_op jit(solution)/shard_map/dot_general | solution.py:15
  116.1 1.6 %copy.8 = f32[128,128]{0,1:T(8,128)} copy(f32[128,128]{1,0:T(8,128)} %fusion.30) | data formatting | bytes 131072 | tf_op jit(solution)/shard_map/dot_general | solution.py:15
  117.7 1.6 %copy.7 = f32[128,128]{0,1:T(8,128)} copy(f32[128,128]{1,0:T(8,128)} %fusion.32) | data formatting | bytes 131072 | tf_op jit(solution)/shard_map/dot_general | solution.py:15
  119.2 2.0 %slice_negate_fusion = (f32[128,128]{0,1:T(8,128)}, f32[128,128]{0,1:T(8,128)}, f32[128,128]{0,1:T(8,128)}) fusion(f32[256,256]{0,1:T(8,128)} %convert_add_fusion, f32[128,128]{1,0:T(8,128)} %fusion.30, f32[128,128]{0,1:T(8,128)} %copy.8, f32[128,128]{0,1:T(8,128)} %copy.7, f32[128,128]{1,0:T(8,128)} %copy-done, f32[128,128]{1,0:T(8,128)} %fusion.32), kind=kOutput, calls=%fused_computation.50 | convolution fusion | flops 25264128 | bytes 720896 | tf_op jit(solution)/shard_map/dot_general | solution.py:15
  121.2 1.6 %copy.9 = f32[128,128]{0,1:T(8,128)} copy(f32[128,128]{1,0:T(8,128)} %bitcast.41) | data formatting | bytes 131072 | tf_op jit(solution)/shard_map/transpose | solution.py:101
  122.8 2.5 %subtract_convert_fusion.1 = bf16[1536,256]{0,1:T(8,128)(2,1)S(1)} fusion(f32[1536,128]{0,1:T(8,128)} %fusion.14, bf16[1536,256]{0,1:T(8,128)(2,1)} %constant_dynamic-update-slice_fusion, bf16[1536,128]{1,0:T(8,128)(2,1)S(1)} %get-tuple-element.10, bf16[1536,128]{1,0:T(8,128)(2,1)} %copy-done.2, f32[128,128]{0,1:T(8,128)} %get-tuple-element.13, ...), kind=kOutput, calls=%fused_computation.12 | convolution fusion | flops 1211301888 | bytes 3407872 | tf_op jit(solution)/shard_map/dot_general | solution.py:15
  125.3 9.9 %subtract_convert_fusion = bf16[1536,3072]{1,0:T(8,128)(2,1)} fusion(bf16[1536,3072]{1,0:T(8,128)(2,1)} %param.2, bf16[3072,256]{0,1:T(8,128)(2,1)S(1)} %constant_dynamic-update-slice_fusion.10, bf16[3072,256]{0,1:T(8,128)(2,1)S(1)} %constant_dynamic-update-slice_fusion.4, bf16[1536,256]{0,1:T(8,128)(2,1)S(1)} %subtract_convert_fusion.1, ...), kind=kOutput, calls=%fused_computation | convolution fusion | flops 4857004032 | bytes 23592960 | tf_op jit(solution)/shard_map/dot_general | solution.py:11
  (53 shorter events, 3.8 us)
Async XLA Ops:
  1.2 14.9 %copy-start.2 = (bf16[1536,128]{1,0:T(8,128)(2,1)}, bf16[1536,128]{1,0:T(8,128)(2,1)S(1)}, u32[]{:S(2)}) copy-start(bf16[1536,128]{1,0:T(8,128)(2,1)S(1)} %get-tuple-element.11) | copy-start | bytes 1179652
  1.2 14.7 %collective-permute-start.2 = (bf16[384,256]{1,0:T(8,128)(2,1)S(1)}, bf16[384,256]{1,0:T(8,128)(2,1)S(1)}, u32[]{:S(2)}, u32[]{:S(2)}) collective-permute-start(bf16[384,256]{1,0:T(8,128)(2,1)S(1)} %fusion.26), channel_id=1, source_target_pairs={{0,16},{1,8},{2,0},{3,24},{4,20},{5,12},{6,4},{7,28},{8,17},{9,9},... | collective-permute-start | bytes 589832 | tf_op jit(solution)/shard_map/ppermute | solution.py:44
  7.2 8.8 %collective-permute-start = (bf16[384,256]{1,0:T(8,128)(2,1)S(1)}, bf16[384,256]{1,0:T(8,128)(2,1)S(1)}, u32[]{:S(2)}, u32[]{:S(2)}) collective-permute-start(bf16[384,256]{1,0:T(8,128)(2,1)S(1)} %fusion.26), channel_id=1, source_target_pairs={{0,0},{1,24},{2,16},{3,8},{4,4},{5,28},{6,20},{7,12},{8,1},{9,25},... | collective-permute-start | bytes 589832 | tf_op jit(solution)/shard_map/ppermute | solution.py:44
  7.9 10.4 %collective-permute-start.1 = (bf16[384,256]{1,0:T(8,128)(2,1)S(1)}, bf16[384,256]{1,0:T(8,128)(2,1)S(1)}, u32[]{:S(2)}, u32[]{:S(2)}) collective-permute-start(bf16[384,256]{1,0:T(8,128)(2,1)S(1)} %fusion.26), channel_id=1, source_target_pairs={{0,8},{1,0},{2,24},{3,16},{4,12},{5,4},{6,28},{7,20},{8,9},{9,1},{... | collective-permute-start | bytes 589832 | tf_op jit(solution)/shard_map/ppermute | solution.py:44
  11.1 8.8 %collective-permute-start.3 = (bf16[384,256]{1,0:T(8,128)(2,1)S(1)}, bf16[384,256]{1,0:T(8,128)(2,1)S(1)}, u32[]{:S(2)}, u32[]{:S(2)}) collective-permute-start(bf16[384,256]{1,0:T(8,128)(2,1)S(1)} %fusion.26), channel_id=1, source_target_pairs={{0,24},{1,16},{2,8},{3,0},{4,28},{5,20},{6,12},{7,4},{8,25},{9,17}... | collective-permute-start | bytes 589832 | tf_op jit(solution)/shard_map/ppermute | solution.py:44
  20.1 2.4 %collective-permute-start.4 = (bf16[1536,256]{0,1:T(8,128)(2,1)S(1)}, bf16[1536,256]{0,1:T(8,128)(2,1)S(1)}, u32[]{:S(2)}, u32[]{:S(2)}) collective-permute-start(bf16[1536,256]{0,1:T(8,128)(2,1)S(1)} %constant_dynamic-update-slice_fusion.12), channel_id=1, source_target_pairs={{0,4},{4,0},{8,12},{12,8},{16,20},{20,16},{24,28},{28,24},{1,5},{5... | collective-permute-start | bytes 2359304 | tf_op jit(solution)/shard_map/ppermute | solution.py:52
  27.8 14.5 %collective-permute-start.8 = (bf16[384,256]{0,1:T(8,128)(2,1)S(1)}, bf16[384,256]{0,1:T(8,128)(2,1)S(1)}, u32[]{:S(2)}, u32[]{:S(2)}) collective-permute-start(bf16[384,256]{0,1:T(8,128)(2,1)S(1)} %get-tuple-element.7), channel_id=1, source_target_pairs={{0,1},{1,2},{2,3},{3,0},{4,5},{5,6},{6,7},{7,4},{8,9},{9,10},{10,1... | collective-permute-start | bytes 589832 | tf_op jit(solution)/shard_map/ppermute | solution.py:75
  36.8 13.1 %collective-permute-start.10 = (bf16[384,256]{0,1:T(8,128)(2,1)S(1)}, bf16[384,256]{0,1:T(8,128)(2,1)S(1)}, u32[]{:S(2)}, u32[]{:S(2)}) collective-permute-start(bf16[384,256]{0,1:T(8,128)(2,1)S(1)} %get-tuple-element.8), channel_id=1, source_target_pairs={{0,3},{1,0},{2,1},{3,2},{4,7},{5,4},{6,5},{7,6},{8,11},{9,8},{10,9... | collective-permute-start | bytes 589832 | tf_op jit(solution)/shard_map/ppermute | solution.py:75
  36.8 13.1 %collective-permute-start.9 = (bf16[384,256]{0,1:T(8,128)(2,1)S(1)}, bf16[384,256]{0,1:T(8,128)(2,1)S(1)}, u32[]{:S(2)}, u32[]{:S(2)}) collective-permute-start(bf16[384,256]{0,1:T(8,128)(2,1)S(1)} %get-tuple-element.9), channel_id=1, source_target_pairs={{0,2},{1,3},{2,0},{3,1},{4,6},{5,7},{6,4},{7,5},{8,10},{9,11},{10,... | collective-permute-start | bytes 589832 | tf_op jit(solution)/shard_map/ppermute | solution.py:75
  41.7 10.8 %collective-permute-start.7 = (f32[128,128]{1,0:T(8,128)S(1)}, f32[128,128]{1,0:T(8,128)S(1)}, u32[]{:S(2)}, u32[]{:S(2)}) collective-permute-start(f32[128,128]{1,0:T(8,128)S(1)} %fusion.11), channel_id=1, source_target_pairs={{0,3},{1,0},{2,1},{3,2},{4,7},{5,4},{6,5},{7,6},{8,11},{9,8},{10,9... | collective-permute-start | bytes 196616 | tf_op jit(solution)/shard_map/ppermute | solution.py:63
  41.7 10.7 %collective-permute-start.6 = (f32[128,128]{1,0:T(8,128)S(1)}, f32[128,128]{1,0:T(8,128)S(1)}, u32[]{:S(2)}, u32[]{:S(2)}) collective-permute-start(f32[128,128]{1,0:T(8,128)S(1)} %fusion.11), channel_id=1, source_target_pairs={{0,2},{1,3},{2,0},{3,1},{4,6},{5,7},{6,4},{7,5},{8,10},{9,11},{10,... | collective-permute-start | bytes 196616 | tf_op jit(solution)/shard_map/ppermute | solution.py:63
  42.4 10.1 %collective-permute-start.5 = (f32[128,128]{1,0:T(8,128)S(1)}, f32[128,128]{1,0:T(8,128)S(1)}, u32[]{:S(2)}, u32[]{:S(2)}) collective-permute-start(f32[128,128]{1,0:T(8,128)S(1)} %fusion.11), channel_id=1, source_target_pairs={{0,1},{1,2},{2,3},{3,0},{4,5},{5,6},{6,7},{7,4},{8,9},{9,10},{10,1... | collective-permute-start | bytes 196616 | tf_op jit(solution)/shard_map/ppermute | solution.py:63
  51.6 29.2 %copy-start.3 = (bf16[2,1536,128]{2,1,0:T(8,128)(2,1)S(1)}, bf16[2,1536,128]{2,1,0:T(8,128)(2,1)}, u32[]{:S(2)}) copy-start(bf16[2,1536,128]{2,1,0:T(8,128)(2,1)} %param.3) | copy-start | bytes 2359300
  51.6 22.5 %collective-permute-start.12 = (bf16[384,256]{0,1:T(8,128)(2,1)S(1)}, bf16[384,256]{0,1:T(8,128)(2,1)S(1)}, u32[]{:S(2)}, u32[]{:S(2)}) collective-permute-start(bf16[384,256]{0,1:T(8,128)(2,1)S(1)} %get-tuple-element.6), channel_id=1, source_target_pairs={{0,8},{1,0},{2,24},{3,16},{4,12},{5,4},{6,28},{7,20},{8,9},{9,1},{... | collective-permute-start | bytes 589832 | tf_op jit(solution)/shard_map/ppermute | solution.py:44
  51.7 11.2 %collective-permute-start.11 = (bf16[384,256]{0,1:T(8,128)(2,1)S(1)}, bf16[384,256]{0,1:T(8,128)(2,1)S(1)}, u32[]{:S(2)}, u32[]{:S(2)}) collective-permute-start(bf16[384,256]{0,1:T(8,128)(2,1)S(1)} %get-tuple-element.6), channel_id=1, source_target_pairs={{0,0},{1,24},{2,16},{3,8},{4,4},{5,28},{6,20},{7,12},{8,1},{9,25},... | collective-permute-start | bytes 589832 | tf_op jit(solution)/shard_map/ppermute | solution.py:44
  52.5 28.3 %copy-start = (f32[128,128]{1,0:T(8,128)}, f32[128,128]{1,0:T(8,128)S(1)}, u32[]{:S(2)}) copy-start(f32[128,128]{1,0:T(8,128)S(1)} %add_add_fusion) | copy-start | bytes 196612
  52.5 32.3 %collective-permute-start.20 = (bf16[384,256]{0,1:T(8,128)(2,1)S(1)}, bf16[384,256]{0,1:T(8,128)(2,1)S(1)}, u32[]{:S(2)}, u32[]{:S(2)}) collective-permute-start(bf16[384,256]{0,1:T(8,128)(2,1)S(1)} %get-tuple-element.6), channel_id=1, source_target_pairs={{0,2},{1,3},{2,0},{3,1},{4,6},{5,7},{6,4},{7,5},{8,10},{9,11},{10,... | collective-permute-start | bytes 589832 | tf_op jit(solution)/shard_map/ppermute | solution.py:84
  57.3 26.8 %collective-permute-start.19 = (bf16[384,256]{0,1:T(8,128)(2,1)S(1)}, bf16[384,256]{0,1:T(8,128)(2,1)S(1)}, u32[]{:S(2)}, u32[]{:S(2)}) collective-permute-start(bf16[384,256]{0,1:T(8,128)(2,1)S(1)} %get-tuple-element.6), channel_id=1, source_target_pairs={{0,1},{1,2},{2,3},{3,0},{4,5},{5,6},{6,7},{7,4},{8,9},{9,10},{10,1... | collective-permute-start | bytes 589832 | tf_op jit(solution)/shard_map/ppermute | solution.py:84
  59.9 20.2 %collective-permute-start.14 = (bf16[384,256]{0,1:T(8,128)(2,1)S(1)}, bf16[384,256]{0,1:T(8,128)(2,1)S(1)}, u32[]{:S(2)}, u32[]{:S(2)}) collective-permute-start(bf16[384,256]{0,1:T(8,128)(2,1)S(1)} %get-tuple-element.6), channel_id=1, source_target_pairs={{0,24},{1,16},{2,8},{3,0},{4,28},{5,20},{6,12},{7,4},{8,25},{9,17}... | collective-permute-start | bytes 589832 | tf_op jit(solution)/shard_map/ppermute | solution.py:44
  62.8 16.6 %collective-permute-start.13 = (bf16[384,256]{0,1:T(8,128)(2,1)S(1)}, bf16[384,256]{0,1:T(8,128)(2,1)S(1)}, u32[]{:S(2)}, u32[]{:S(2)}) collective-permute-start(bf16[384,256]{0,1:T(8,128)(2,1)S(1)} %get-tuple-element.6), channel_id=1, source_target_pairs={{0,16},{1,8},{2,0},{3,24},{4,20},{5,12},{6,4},{7,28},{8,17},{9,9},... | collective-permute-start | bytes 589832 | tf_op jit(solution)/shard_map/ppermute | solution.py:44
  80.8 19.1 %collective-permute-start.15 = (bf16[1536,256]{0,1:T(8,128)(2,1)}, bf16[1536,256]{0,1:T(8,128)(2,1)}, u32[]{:S(2)}, u32[]{:S(2)}) collective-permute-start(bf16[1536,256]{0,1:T(8,128)(2,1)} %constant_dynamic-update-slice_fusion.6), channel_id=1, source_target_pairs={{0,4},{4,0},{8,12},{12,8},{16,20},{20,16},{24,28},{28,24},{1,5},{5... | collective-permute-start | bytes 2359304 | tf_op jit(solution)/shard_map/ppermute | solution.py:52
  82.3 15.5 %collective-permute-start.21 = (bf16[384,256]{0,1:T(8,128)(2,1)S(1)}, bf16[384,256]{0,1:T(8,128)(2,1)S(1)}, u32[]{:S(2)}, u32[]{:S(2)}) collective-permute-start(bf16[384,256]{0,1:T(8,128)(2,1)S(1)} %get-tuple-element.6), channel_id=1, source_target_pairs={{0,3},{1,0},{2,1},{3,2},{4,7},{5,4},{6,5},{7,6},{8,11},{9,8},{10,9... | collective-permute-start | bytes 589832 | tf_op jit(solution)/shard_map/ppermute | solution.py:84
  101.2 4.8 %copy-start.1 = (f32[128,128]{1,0:T(8,128)S(1)}, f32[128,128]{1,0:T(8,128)}, u32[]{:S(2)}) copy-start(f32[128,128]{1,0:T(8,128)} %copy-done) | copy-start | bytes 196612
  101.8 6.6 %collective-permute-start.18 = (bf16[256,256]{0,1:T(8,128)(2,1)S(1)}, bf16[256,256]{0,1:T(8,128)(2,1)S(1)}, u32[]{:S(2)}, u32[]{:S(2)}) collective-permute-start(bf16[256,256]{0,1:T(8,128)(2,1)S(1)} %get-tuple-element.17), channel_id=1, source_target_pairs={{0,3},{1,0},{2,1},{3,2},{4,7},{5,4},{6,5},{7,6},{8,11},{9,8},{10,9... | collective-permute-start | bytes 393224 | tf_op jit(solution)/shard_map/ppermute | solution.py:63
  101.9 9.2 %collective-permute-start.17 = (bf16[256,256]{0,1:T(8,128)(2,1)S(1)}, bf16[256,256]{0,1:T(8,128)(2,1)S(1)}, u32[]{:S(2)}, u32[]{:S(2)}) collective-permute-start(bf16[256,256]{0,1:T(8,128)(2,1)S(1)} %get-tuple-element.17), channel_id=1, source_target_pairs={{0,2},{1,3},{2,0},{3,1},{4,6},{5,7},{6,4},{7,5},{8,10},{9,11},{10,... | collective-permute-start | bytes 393224 | tf_op jit(solution)/shard_map/ppermute | solution.py:63
  106.0 5.9 %collective-permute-start.16 = (bf16[256,256]{0,1:T(8,128)(2,1)S(1)}, bf16[256,256]{0,1:T(8,128)(2,1)S(1)}, u32[]{:S(2)}, u32[]{:S(2)}) collective-permute-start(bf16[256,256]{0,1:T(8,128)(2,1)S(1)} %get-tuple-element.17), channel_id=1, source_target_pairs={{0,1},{1,2},{2,3},{3,0},{4,5},{5,6},{6,7},{7,4},{8,9},{9,10},{10,1... | collective-permute-start | bytes 393224 | tf_op jit(solution)/shard_map/ppermute | solution.py:63
  122.8 2.5 %copy-start.4 = (bf16[1536,128]{0,1:T(8,128)(2,1)S(1)}, bf16[1536,128]{0,1:T(8,128)(2,1)}, u32[]{:S(2)}) copy-start(bf16[1536,128]{0,1:T(8,128)(2,1)} %copy.11) | copy-start | bytes 1179652
  122.8 2.6 %copy-start.5 = (bf16[1536,128]{0,1:T(8,128)(2,1)S(1)}, bf16[1536,128]{0,1:T(8,128)(2,1)}, u32[]{:S(2)}) copy-start(bf16[1536,128]{0,1:T(8,128)(2,1)} %copy.10) | copy-start | bytes 1179652

commit v2 on v0

v2 whole, which is shorter than its diff:
```python
import functools

import jax
import jax.numpy as jnp
from jax import lax
from jax.experimental import pallas as pl
from jax.experimental.pallas import tpu as pltpu
from jax.sharding import PartitionSpec as P


F32 = jnp.float32
BF16 = jnp.bfloat16
WHOLE = pl.BlockSpec(memory_space=pltpu.VMEM)


def params(mib):
    return pltpu.CompilerParams(vmem_limit_bytes=mib * 2**20)


def dot(a, b, ca=1, cb=0):
    return lax.dot_general(a, b, (((ca,), (cb,)), ((), ())), preferred_element_type=F32)


def exact(a, b):
    return lax.dot_general(
        a, b, (((1,), (0,)), ((), ())), precision=lax.Precision.HIGHEST, preferred_element_type=F32
    )


def halves(x):
    hi = x.astype(BF16)
    return hi, (x - hi.astype(F32)).astype(BF16)


def rows_at(index, part):
    return pl.ds(pl.multiple_of(index * part, part), part)


def sizes():
    rows = lax.axis_size("row")
    cols = lax.axis_size("col")
    return cols, rows // cols


def place():
    _, ratio = sizes()
    row = lax.axis_index("row")
    return lax.div(row, ratio), lax.rem(row, ratio), lax.axis_index("col")


def call(kernel, ins, outs, mib=8, **kw):
    return pl.pallas_call(
        kernel,
        in_specs=[WHOLE] * len(ins),
        out_specs=[WHOLE] * len(outs),
        out_shape=[jax.ShapeDtypeStruct(*out) for out in outs],
        compiler_params=params(mib),
        **kw,
    )(*ins)


def split_kernel(panels_ref, *pieces):
    _, _, col = place()
    for n, piece in enumerate(pieces):
        piece[...] = panels_ref[n, rows_at(col, piece.shape[0]), :]


def split(panels):
    cols, _ = sizes()
    n_panels, n_rows, b = panels.shape
    return call(split_kernel, [panels], [((n_rows // cols, b), BF16)] * n_panels)


def gate_kernel(x_ref, *refs):
    refs[-1][...] = x_ref[...]


def gate(x, *after):
    return call(gate_kernel, [x, *after], [(x.shape, BF16)])[0]


def load_kernel(a_ref, *refs):
    out_ref, sem = refs[-2:]
    copy = pltpu.make_async_copy(a_ref, out_ref, sem)
    copy.start()
    copy.wait()


def load(a_tile, *after):
    return pl.pallas_call(
        load_kernel,
        in_specs=[pl.BlockSpec(memory_space=pl.ANY)] + [WHOLE] * len(after),
        out_specs=WHOLE,
        out_shape=jax.ShapeDtypeStruct(a_tile.shape, BF16),
        scratch_shapes=[pltpu.SemaphoreType.DMA],
        compiler_params=params(44),
        name="load",
    )(a_tile, *after)


def pick_kernel(after_ref, *refs, cols):
    del after_ref
    group, _, col = place()
    for o in range(cols):
        source = jnp.bitwise_xor(group, jnp.bitwise_xor(col, o))
        for d in range(cols):

            @pl.when(source == d)
            def _(o=o, d=d):
                refs[cols + o][...] = refs[d][...]


def pick(after, pieces):
    cols = len(pieces)
    kernel = functools.partial(pick_kernel, cols=cols)
    return call(kernel, [after, *pieces], [(pieces[0].shape, BF16)] * cols)


def join_kernel(*refs, cols):
    _, _, col = place()
    out = refs[-1]
    part = refs[0].shape[0]
    for o, piece in enumerate(refs[:cols]):
        out[rows_at(jnp.bitwise_xor(col, o), part), :] = piece[...]


def join(pieces, *after):
    part, width = pieces[0].shape
    cols = len(pieces)
    kernel = functools.partial(join_kernel, cols=cols)
    return call(kernel, [*pieces, *after], [((cols * part, width), BF16)])[0]


def product_kernel(after_ref, a_ref, *refs, cols, ratio, extra):
    del after_ref
    blocks = refs[:ratio]
    others = refs[ratio : (2 if extra else 1) * ratio]
    outs = refs[ratio + len(others) :]
    _, member, col = place()
    length = blocks[0].shape[0]
    part = outs[0].shape[0]
    for o in [*range(1, cols), 0]:
        rows = rows_at(jnp.bitwise_xor(col, o), part)
        value = dot(a_ref[rows, rows_at(member, length)], blocks[0][...])
        for m in range(1, ratio):
            at = lax.rem(member + m, ratio)
            value = value + dot(a_ref[rows, rows_at(at, length)], blocks[m][...])
        outs[o][...] = value.astype(outs[o].dtype)
    if extra:
        s = dot(others[0][...], blocks[0][...], 0, 0)
        for m in range(1, ratio):
            s = s + dot(others[m][...], blocks[m][...], 0, 0)
        outs[cols][...] = s


def product(after, a_tile, blocks, others=()):
    cols, ratio = sizes()
    b = blocks[0].shape[1]
    part = a_tile.shape[0] // cols
    outs = [((part, b), F32)] + [((part, b), BF16)] * (cols - 1)
    if others:
        outs.append(((b, b), F32))
    kernel = functools.partial(product_kernel, cols=cols, ratio=ratio, extra=bool(others))
    return call(kernel, [after, a_tile, *blocks, *others], outs, 16)


def total_kernel(own_ref, after_ref, *refs, count):
    del after_ref
    value = own_ref[...]
    for got in refs[:count]:
        value = value + got[...].astype(F32)
    piece = value.astype(BF16)
    if len(refs) > count + 1:
        s_ref, piece_ref, wire_ref = refs[count:]
        part = own_ref.shape[0]
        piece_ref[...] = piece
        wire_ref[:part, :] = piece
        wire_ref[part:, :] = s_ref[...].astype(BF16)
    else:
        refs[-1][...] = piece


def total(own, got, after, *s):
    part, b = own.shape
    outs = [(own.shape, BF16)] + [((part + b, b), BF16)] * len(s)
    kernel = functools.partial(total_kernel, count=len(got))
    return call(kernel, [own, after, *got, *s], outs)


def gram_kernel(*refs, ratio):
    v1, v2, p1, p2 = (refs[n * ratio : (n + 1) * ratio] for n in range(4))
    own_ref, wire_ref = refs[4 * ratio :]
    for n, (left, right) in enumerate(((v1, p1), (v1, p2), (v2, p2))):
        g = dot(left[0][...], right[0][...], 0, 0)
        for m in range(1, ratio):
            g = g + dot(left[m][...], right[m][...], 0, 0)
        own_ref[n] = g
        wire_ref[n] = g.astype(BF16)


def gram(v1, v2, p1, p2):
    b = v1[0].shape[1]
    outs = [((3, b, b), F32), ((3, b, b), BF16)]
    return call(functools.partial(gram_kernel, ratio=len(v1)), [*v1, *v2, *p1, *p2], outs)


def pack_kernel(after_ref, panels_ref, s_ref, *refs, ratio, cols, b):
    del after_ref
    parts = [refs[n * ratio : (n + 1) * ratio] for n in range(4)]
    firsts = refs[4 * ratio : 4 * ratio + cols]
    seconds = refs[4 * ratio + cols : 4 * ratio + 2 * cols]
    rights = refs[4 * ratio + 2 * cols : 5 * ratio + 2 * cols]
    x_ref, y_ref, s_out = refs[5 * ratio + 2 * cols :]
    _, _, col = place()
    for m in range(ratio):
        for n in range(4):
            rights[m][:, n * b : (n + 1) * b] = parts[n][m][...]
    part = seconds[0].shape[0]
    s = s_ref[...]
    for wire in firsts[1:]:
        s = s + wire[part:, :].astype(F32)
    s_out[...] = s
    s_hi, s_lo = halves(s)
    st_hi, st_lo = halves(s.T)
    v1 = panels_ref[0]
    v2 = panels_ref[1]
    x_ref[:, :b] = (v1.astype(F32) - (dot(v2, st_hi) + dot(v2, st_lo))).astype(BF16)
    x_ref[:, b:] = v2
    for o in range(cols):
        rows = rows_at(jnp.bitwise_xor(col, o), part)
        p1 = firsts[o][:part, :]
        y_ref[rows, :b] = p1.astype(F32)
        y_ref[rows, b:] = seconds[o][...].astype(F32) - (dot(p1, s_hi) + dot(p1, s_lo))


def pack(after, panels, s, p1, p2, v1, v2, firsts, seconds):
    _, n_rows, b = panels.shape
    ratio = len(v1)
    cols = len(firsts)
    outs = [((n_rows, 4 * b), BF16)] * ratio + [((n_rows, 2 * b), BF16), ((n_rows, 2 * b), F32), ((b, b), F32)]
    kernel = functools.partial(pack_kernel, ratio=ratio, cols=cols, b=b)
    ins = [after, panels, s, *p1, *p2, *v1, *v2, *firsts, *seconds]
    out = call(kernel, ins, outs, 16)
    return out[:ratio], *out[ratio:]


def update_kernel(a_ref, panels_ref, x_ref, y_ref, s_ref, own, *refs, ratio, per, cols, b):
    wires = refs[: cols - 1]
    rights = refs[cols - 1 : cols - 1 + ratio]
    out_ref, left_ref, slots, sems = refs[cols - 1 + ratio :]
    width = 2 * b
    block = slots.shape[2]
    _, member, _ = place()

    total = own[...]
    for wire in wires:
        total = total + wire[...].astype(F32)
    c1, g12, g22 = total[0], total[1], total[2]
    s = s_ref[...]
    k12 = exact(c1, s) - g12
    c2 = g22 + exact(s.T, k12) - exact(g12.T, s)
    top_hi, top_lo = halves(jnp.concatenate([-c1, k12], axis=1))
    low_hi, low_lo = halves(jnp.concatenate([k12.T, -c2], axis=1))
    v1 = panels_ref[0]
    v2 = panels_ref[1]
    y = y_ref[...] + (dot(v1, top_hi) + dot(v2, low_hi)) + (dot(v1, top_lo) + dot(v2, low_lo))
    left_ref[:, :width] = x_ref[...]
    left_ref[:, width:] = y.astype(BF16)

    copies = []
    for m in range(ratio):
        for j in range(per):
            n = m * per + j
            start = pl.multiple_of((lax.rem(member + m, ratio) * per + j) * block, block)
            if n >= 2:
                copies[n - 2].wait()
            change = dot(left_ref[...], rights[m][j * block : (j + 1) * block, :], 1, 1)
            now = a_ref[:, pl.ds(start, block)].astype(F32)
            slots[n % 2] = (now - change).astype(BF16)
            copies.append(
                pltpu.make_async_copy(slots.at[n % 2], out_ref.at[:, pl.ds(start, block)], sems.at[n % 2])
            )
            copies[n].start()
    for copy in copies[-2:]:
        copy.wait()


def update(a_tile, panels, x, y, s, own, wires, rights, block):
    n_rows, n_cols = a_tile.shape
    ratio = len(rights)
    length, width = rights[0].shape
    cols = len(wires) + 1
    per = length // block
    return pl.pallas_call(
        functools.partial(update_kernel, ratio=ratio, per=per, cols=cols, b=width // 4),
        in_specs=[WHOLE] * (5 + cols + ratio),
        out_specs=pl.BlockSpec(memory_space=pl.ANY),
        scratch_shapes=[
            pltpu.VMEM((n_rows, width), BF16),
            pltpu.VMEM((2, n_rows, block), BF16),
            pltpu.SemaphoreType.DMA((2,)),
        ],
        out_shape=jax.ShapeDtypeStruct((n_rows, n_cols), BF16),
        compiler_params=params(24),
        name="update",
    )(a_tile, panels, x, y, s, own, *wires, *rights)


def body(a_tile, panels):
    cols, ratio = sizes()

    def across(x, o):
        return lax.ppermute(x, "col", [(c, c ^ o) for c in range(cols)])

    def along(x, d):
        pairs = [(g * ratio + m, (g ^ d) * ratio + m) for g in range(cols) for m in range(ratio)]
        return lax.ppermute(x, "row", pairs)

    def share(x):
        got = [x]
        for o in range(1, ratio):
            pairs = [(g * ratio + m, g * ratio + (m - o) % ratio) for g in range(cols) for m in range(ratio)]
            got.append(lax.ppermute(x, "row", pairs))
        return got

    def gather(x):
        pieces = {0: x}
        step = cols // 2
        while step:
            for d in list(pieces):
                pieces[d | step] = along(pieces[d], step)
            step //= 2
        return [pieces[d] for d in range(cols)]

    def trade(kept, *sent):
        return [kept] + [across(sent[o - 1], o) for o in range(1, cols)]

    piece1, piece2 = split(panels)
    tile = load(a_tile, piece1)
    far1 = gather(piece1)
    piece2 = gate(piece2, far1[cols // 2])
    far2 = gather(piece2)
    picked1 = pick(piece2, far1)
    block1 = join(trade(*picked1), tile)
    v1 = share(block1)
    picked2 = pick(block1, far2)
    own1, *sent1 = product(picked2[0], tile, v1)
    block2 = join(trade(*picked2), own1)
    v2 = share(block2)
    *out2, s_own = product(block2, tile, v2, v1)
    own2, *sent2 = out2

    piece1, wire1 = total(own1, trade(own1, *sent1)[1:], own2, s_own)
    far1 = gather(piece1)
    firsts = trade(*[wire1] * cols)
    piece2 = total(own2, trade(own2, *sent2)[1:], piece1)[0]
    far2 = gather(piece2)
    seconds = trade(*[piece2] * cols)
    picked1 = pick(piece2, far1)
    picked2 = pick(picked1[0], far2)
    block1 = join(trade(*picked1), picked2[0])
    p1 = share(block1)
    block2 = join(trade(*picked2), block1)
    p2 = share(block2)
    own, gwire = gram(v1, v2, p1, p2)
    gwires = trade(*[gwire] * cols)[1:]
    rights, x, y, s = pack(own, panels, s_own, p1, p2, v1, v2, firsts, seconds)
    return update(tile, panels, x, y, s, own, gwires, rights, 512)


def solution(mesh):
    in_specs = (P("row", "col"), P(None, "row", None))
    out_specs = P("row", "col")
    return jax.shard_map(body, mesh=mesh, in_specs=in_specs, out_specs=out_specs, check_vma=False)
```

time: 394 us -> 109 us (0.28)
  waiting for transfers between devices: 221 us -> 33.5 us
  matrix products: 68.3 us -> 0 us
  blocking collectives: 60.1 us -> 0 us
  starting transfers between devices: 0.29 us -> 52 us
  local copies, waits for them, and re-layouts: 26.3 us -> 1.14 us
  Pallas kernels: 0 us -> 21.5 us
  between operations: 13.6 us -> 0.36 us
  other arithmetic: 4.14 us -> 0 us
    psum x2 -> x0, waiting for transfers between devices: 82.9 us -> none  [spread(): return lax.psum(block, axis)]
    reduce_scatter x2 -> x0, waiting for transfers between devices: 70.1 us -> none  [per_device(): lax.psum_scatter(lax.dot_general(tile_now, v_rows, (((0,), (0,)), ((), ()...]
    dot_general x12 -> x0, matrix products: 68.3 us -> none  [the longest x2 29.4 us: per_device(): lax.dot_general(w_rows, v_cols, (((1,), (1,)), ((), ())), preferred_eleme...]
    all_gather x4 -> x0, waiting for transfers between devices: 66.8 us -> none  [the longest x2 50.3 us: per_device(): av_cols = lax.all_gather(av_fine, 'row', axis=0, tiled=True)]
    psum x2 -> x0, blocking collectives: 60.1 us -> none  [per_device(): lax.psum(local_sum.astype(jnp.bfloat16), 'row').astype(jnp.float32)]
    ppermute x0 -> x43, starting transfers between devices: none -> 52 us  [the longest x27 31.3 us: across(): return lax.ppermute(x, 'col', [(c, c ^ o) for c in range(cols)])]
    ppermute x0 -> x43, waiting for transfers between devices: none -> 33.5 us  [the longest x12 18.5 us: along(): return lax.ppermute(x, 'row', pairs)]
    pallas_call x0 -> x18, Pallas kernels: none -> 21.5 us  [the longest x1 9.69 us: update(): pl.pallas_call(functools.partial(update_kernel, ratio=ratio, per=per, col...]
  transfers between devices with their start and end apart: 8 -> 43, of which waited for: 8 -> 21; matrix products, arithmetic and copies ran while one was open for 4% -> 0% of each run, Pallas kernels for 0% -> 11%
where the time goes in v2:
time: 109 us; the launch traced here: 108 us
  starting transfers between devices  52 us (48%)
  waiting for transfers between devices  33.5 us (31%)
  Pallas kernels  21.5 us (20%)
  local copies, waits for them, and re-layouts  1.14 us (1%)
    ppermute x27, starting transfers between devices, across(): return lax.ppermute(x, 'col', [(c, c ^ o) for c in range(cols)])  31.3 us
    ppermute x12, starting transfers between devices, along(): return lax.ppermute(x, 'row', pairs)  20.4 us
    ppermute x12, waiting for transfers between devices, along(): return lax.ppermute(x, 'row', pairs)  18.5 us
    ppermute x27, waiting for transfers between devices, across(): return lax.ppermute(x, 'col', [(c, c ^ o) for c in range(cols)])  15 us
    pallas_call x1, Pallas kernels, update(): pl.pallas_call(functools.partial(update_kernel, ratio=ratio, per=per, col...  9.69 us
    pallas_call x16, Pallas kernels, call(): pl.pallas_call(kernel, in_specs=[WHOLE] * len(ins), out_specs=[WHOLE] * l...  8.11 us
    pallas_call x1, Pallas kernels, load(): pl.pallas_call(load_kernel, in_specs=[pl.BlockSpec(memory_space=pl.ANY)]...  3.69 us
  transfers between devices with their start and end apart: 43, of which 21 were waited for; matrix products, arithmetic and copies ran while one was open for 0% of the time, Pallas kernels for 11%

profile of v2, /device:TPU:0, one launch (start us, length us, event | category | flops | bytes accessed | tf_op | source)
XLA Modules:
  0.0 108.5 jit_solution(10932255782210442650)
XLA Ops:
  0.0 1.1 %copy-done = bf16[2,1536,128]{2,1,0:T(8,128)(2,1)S(1)} copy-done((bf16[2,1536,128]{2,1,0:T(8,128)(2,1)S(1)}, bf16[2,1536,128]{2,1,0:T(8,128)(2,1)}, u32[]{:S(2)}) %copy-start) | copy-done | bytes 786456
  1.2 4.1 %collective-permute-start = (bf16[384,128]{1,0:T(8,128)(2,1)S(1)}, bf16[384,128]{1,0:T(8,128)(2,1)S(1)}, u32[]{:S(2)}, u32[]{:S(2)}) collective-permute-start(bf16[384,128]{1,0:T(8,128)(2,1)S(1)} %get-tuple-element.41.refs_0_), channel_id=1, source_target_pairs={{0,16},{4,20},{8,24},{12,28},{16,0},{20,4},{24,8},{28,12},{1,17},{... | collective-permute-start | bytes 294920 | tf_op jit(solution)/shard_map/ppermute | solution.py:317
  5.3 1.6 %collective-permute-start.1 = (bf16[384,128]{1,0:T(8,128)(2,1)S(1)}, bf16[384,128]{1,0:T(8,128)(2,1)S(1)}, u32[]{:S(2)}, u32[]{:S(2)}) collective-permute-start(bf16[384,128]{1,0:T(8,128)(2,1)S(1)} %get-tuple-element.41.refs_0_), channel_id=1, source_target_pairs={{0,8},{4,12},{8,0},{12,4},{16,24},{20,28},{24,16},{28,20},{1,9},{5... | collective-permute-start | bytes 294920 | tf_op jit(solution)/shard_map/ppermute | solution.py:317
  6.9 3.2 %collective-permute-done.refs_0_.refs_2_ = bf16[384,128]{1,0:T(8,128)(2,1)S(1)} collective-permute-done((bf16[384,128]{1,0:T(8,128)(2,1)S(1)}, bf16[384,128]{1,0:T(8,128)(2,1)S(1)}, u32[]{:S(2)}, u32[]{:S(2)}) %collective-permute-start) | collective-permute-done | bytes 98336 | tf_op jit(solution)/shard_map/ppermute | solution.py:317
  10.9 3.8 %collective-permute-done.2.refs_3_ = bf16[384,128]{1,0:T(8,128)(2,1)S(1)} collective-permute-done((bf16[384,128]{1,0:T(8,128)(2,1)S(1)}, bf16[384,128]{1,0:T(8,128)(2,1)S(1)}, u32[]{:S(2)}, u32[]{:S(2)}) %collective-permute-start.2) | collective-permute-done | bytes 98336 | tf_op jit(solution)/shard_map/ppermute | solution.py:317
  14.8 1.8 %collective-permute-start.3 = (bf16[384,128]{1,0:T(8,128)(2,1)S(1)}, bf16[384,128]{1,0:T(8,128)(2,1)S(1)}, u32[]{:S(2)}, u32[]{:S(2)}) collective-permute-start(bf16[384,128]{1,0:T(8,128)(2,1)S(1)} %get-tuple-element.44), channel_id=1, source_target_pairs={{0,1},{1,0},{2,3},{3,2},{4,5},{5,4},{6,7},{7,6},{8,9},{9,8},{10,11... | collective-permute-start | bytes 294920 | tf_op jit(solution)/shard_map/ppermute | solution.py:313
  16.6 1.5 %collective-permute-start.4 = (bf16[384,128]{1,0:T(8,128)(2,1)S(1)}, bf16[384,128]{1,0:T(8,128)(2,1)S(1)}, u32[]{:S(2)}, u32[]{:S(2)}) collective-permute-start(bf16[384,128]{1,0:T(8,128)(2,1)S(1)} %get-tuple-element.45), channel_id=1, source_target_pairs={{0,2},{1,3},{2,0},{3,1},{4,6},{5,7},{6,4},{7,5},{8,10},{9,11},{10,... | collective-permute-start | bytes 294920 | tf_op jit(solution)/shard_map/ppermute | solution.py:313
  18.3 3.7 %load.1.refs_4_.a_ref = bf16[1536,3072]{1,0:T(8,128)(2,1)S(1)} custom-call(bf16[1536,3072]{1,0:T(8,128)(2,1)} %a_ref.1, bf16[384,128]{1,0:T(8,128)(2,1)S(1)} %get-tuple-element.41.refs_0_), custom_call_target="tpu_custom_call" | custom-call | tf_op jit(solution)/shard_map/load/pallas_call | solution.py:90
  22.1 1.6 %collective-permute-done.5.refs_3_ = bf16[384,128]{1,0:T(8,128)(2,1)S(1)} collective-permute-done((bf16[384,128]{1,0:T(8,128)(2,1)S(1)}, bf16[384,128]{1,0:T(8,128)(2,1)S(1)}, u32[]{:S(2)}, u32[]{:S(2)}) %collective-permute-start.5) | collective-permute-done | bytes 98336 | tf_op jit(solution)/shard_map/ppermute | solution.py:313
  23.7 2.4 %collective-permute-start.8 = (bf16[384,128]{1,0:T(8,128)(2,1)S(1)}, bf16[384,128]{1,0:T(8,128)(2,1)S(1)}, u32[]{:S(2)}, u32[]{:S(2)}) collective-permute-start(bf16[384,128]{1,0:T(8,128)(2,1)S(1)} %shard_map.29.after_ref.refs_0_), channel_id=1, source_target_pairs={{0,16},{4,20},{8,24},{12,28},{16,0},{20,4},{24,8},{28,12},{1,17},{... | collective-permute-start | bytes 294920 | tf_op jit(solution)/shard_map/ppermute | solution.py:317
  26.1 1.7 %collective-permute-start.7 = (bf16[384,128]{1,0:T(8,128)(2,1)S(1)}, bf16[384,128]{1,0:T(8,128)(2,1)S(1)}, u32[]{:S(2)}, u32[]{:S(2)}) collective-permute-start(bf16[384,128]{1,0:T(8,128)(2,1)S(1)} %shard_map.29.after_ref.refs_0_), channel_id=1, source_target_pairs={{0,8},{4,12},{8,0},{12,4},{16,24},{20,28},{24,16},{28,20},{1,9},{5... | collective-permute-start | bytes 294920 | tf_op jit(solution)/shard_map/ppermute | solution.py:317
  27.9 4.2 %collective-permute-done.8.refs_2_ = bf16[384,128]{1,0:T(8,128)(2,1)S(1)} collective-permute-done((bf16[384,128]{1,0:T(8,128)(2,1)S(1)}, bf16[384,128]{1,0:T(8,128)(2,1)S(1)}, u32[]{:S(2)}, u32[]{:S(2)}) %collective-permute-start.8) | collective-permute-done | bytes 98336 | tf_op jit(solution)/shard_map/ppermute | solution.py:317
  32.4 4.3 %collective-permute-done.9.refs_3_ = bf16[384,128]{1,0:T(8,128)(2,1)S(1)} collective-permute-done((bf16[384,128]{1,0:T(8,128)(2,1)S(1)}, bf16[384,128]{1,0:T(8,128)(2,1)S(1)}, u32[]{:S(2)}, u32[]{:S(2)}) %collective-permute-start.9) | collective-permute-done | bytes 98336 | tf_op jit(solution)/shard_map/ppermute | solution.py:317
  37.3 1.2 %collective-permute-start.11 = (bf16[384,128]{1,0:T(8,128)(2,1)S(1)}, bf16[384,128]{1,0:T(8,128)(2,1)S(1)}, u32[]{:S(2)}, u32[]{:S(2)}) collective-permute-start(bf16[384,128]{1,0:T(8,128)(2,1)S(1)} %get-tuple-element.49), channel_id=1, source_target_pairs={{0,2},{1,3},{2,0},{3,1},{4,6},{5,7},{6,4},{7,5},{8,10},{9,11},{10,... | collective-permute-start | bytes 294920 | tf_op jit(solution)/shard_map/ppermute | solution.py:313
  38.5 1.8 %collective-permute-start.12 = (bf16[384,128]{1,0:T(8,128)(2,1)S(1)}, bf16[384,128]{1,0:T(8,128)(2,1)S(1)}, u32[]{:S(2)}, u32[]{:S(2)}) collective-permute-start(bf16[384,128]{1,0:T(8,128)(2,1)S(1)} %get-tuple-element.50), channel_id=1, source_target_pairs={{0,3},{1,2},{2,1},{3,0},{4,7},{5,6},{6,5},{7,4},{8,11},{9,10},{10,... | collective-permute-start | bytes 294920 | tf_op jit(solution)/shard_map/ppermute | solution.py:313
  40.3 2.6 %shard_map.33 = (f32[384,128]{1,0:T(8,128)S(1)}, bf16[384,128]{1,0:T(8,128)(2,1)S(1)}, bf16[384,128]{1,0:T(8,128)(2,1)S(1)}, bf16[384,128]{1,0:T(8,128)(2,1)S(1)}) custom-call(bf16[384,128]{1,0:T(8,128)(2,1)S(1)} %get-tuple-element.47.after_ref.refs_0_, bf16[1536,3072]{1,0:T(8,128)(2,1)S(1)} %load.1.refs_4_.a_ref, ...), custom_call_target="tpu_custom_call" | custom-call | tf_op jit(solution)/shard_map/pallas_call | solution.py:52
  42.9 1.1 %collective-permute-done.12.refs_3_ = bf16[384,128]{1,0:T(8,128)(2,1)S(1)} collective-permute-done((bf16[384,128]{1,0:T(8,128)(2,1)S(1)}, bf16[384,128]{1,0:T(8,128)(2,1)S(1)}, u32[]{:S(2)}, u32[]{:S(2)}) %collective-permute-start.12) | collective-permute-done | bytes 98336 | tf_op jit(solution)/shard_map/ppermute | solution.py:313
  45.0 1.5 %collective-permute-start.15 = (bf16[384,128]{1,0:T(8,128)(2,1)S(1)}, bf16[384,128]{1,0:T(8,128)(2,1)S(1)}, u32[]{:S(2)}, u32[]{:S(2)}) collective-permute-start(bf16[384,128]{1,0:T(8,128)(2,1)S(1)} %get-tuple-element.54), channel_id=1, source_target_pairs={{0,2},{1,3},{2,0},{3,1},{4,6},{5,7},{6,4},{7,5},{8,10},{9,11},{10,... | collective-permute-start | bytes 294920 | tf_op jit(solution)/shard_map/ppermute | solution.py:313
  46.5 1.1 %collective-permute-start.16 = (bf16[384,128]{1,0:T(8,128)(2,1)S(1)}, bf16[384,128]{1,0:T(8,128)(2,1)S(1)}, u32[]{:S(2)}, u32[]{:S(2)}) collective-permute-start(bf16[384,128]{1,0:T(8,128)(2,1)S(1)} %get-tuple-element.55), channel_id=1, source_target_pairs={{0,3},{1,2},{2,1},{3,0},{4,7},{5,6},{6,5},{7,4},{8,11},{9,10},{10,... | collective-permute-start | bytes 294920 | tf_op jit(solution)/shard_map/ppermute | solution.py:313
  47.7 2.8 %shard_map.35 = (f32[384,128]{1,0:T(8,128)S(1)}, bf16[384,128]{1,0:T(8,128)(2,1)S(1)}, bf16[384,128]{1,0:T(8,128)(2,1)S(1)}, bf16[384,128]{1,0:T(8,128)(2,1)S(1)}, f32[128,128]{1,0:T(8,128)S(1)}) custom-call(bf16[1536,128]{1,0:T(8,128)(2,1)S(1)} %shard_map.34.after_ref.refs_0_.refs_2_.refs_6_, bf16[1536,3072]{1,0:T(8,128)(2,1)S(1)} %load.1.refs_4_.a_ref, ...), custom_call_target="tpu_custom_call" | custom-call | tf_op jit(solution)/shard_map/pallas_call | solution.py:52
  50.5 0.9 collective-permute-start.17
  51.4 1.5 %collective-permute-start.18 = (bf16[384,128]{1,0:T(8,128)(2,1)S(1)}, bf16[384,128]{1,0:T(8,128)(2,1)S(1)}, u32[]{:S(2)}, u32[]{:S(2)}) collective-permute-start(bf16[384,128]{1,0:T(8,128)(2,1)S(1)} %get-tuple-element.59), channel_id=1, source_target_pairs={{0,2},{1,3},{2,0},{3,1},{4,6},{5,7},{6,4},{7,5},{8,10},{9,11},{10,... | collective-permute-start | bytes 294920 | tf_op jit(solution)/shard_map/ppermute | solution.py:313
  52.9 1.1 %collective-permute-start.19 = (bf16[384,128]{1,0:T(8,128)(2,1)S(1)}, bf16[384,128]{1,0:T(8,128)(2,1)S(1)}, u32[]{:S(2)}, u32[]{:S(2)}) collective-permute-start(bf16[384,128]{1,0:T(8,128)(2,1)S(1)} %get-tuple-element.60), channel_id=1, source_target_pairs={{0,3},{1,2},{2,1},{3,0},{4,7},{5,6},{6,5},{7,4},{8,11},{9,10},{10,... | collective-permute-start | bytes 294920 | tf_op jit(solution)/shard_map/ppermute | solution.py:313
  54.1 2.2 %collective-permute-start.21 = (bf16[384,128]{1,0:T(8,128)(2,1)S(1)}, bf16[384,128]{1,0:T(8,128)(2,1)S(1)}, u32[]{:S(2)}, u32[]{:S(2)}) collective-permute-start(bf16[384,128]{1,0:T(8,128)(2,1)S(1)} %get-tuple-element.57.after_ref.refs_0_), channel_id=1, source_target_pairs={{0,16},{4,20},{8,24},{12,28},{16,0},{20,4},{24,8},{28,12},{1,17},{... | collective-permute-start | bytes 294920 | tf_op jit(solution)/shard_map/ppermute | solution.py:317
  57.1 1.4 %collective-permute-done.19.refs_2_ = bf16[384,128]{1,0:T(8,128)(2,1)S(1)} collective-permute-done((bf16[384,128]{1,0:T(8,128)(2,1)S(1)}, bf16[384,128]{1,0:T(8,128)(2,1)S(1)}, u32[]{:S(2)}, u32[]{:S(2)}) %collective-permute-start.19) | collective-permute-done | bytes 98336 | tf_op jit(solution)/shard_map/ppermute | solution.py:313
  58.5 2.3 %collective-permute-start.27 = (bf16[384,128]{1,0:T(8,128)(2,1)S(1)}, bf16[384,128]{1,0:T(8,128)(2,1)S(1)}, u32[]{:S(2)}, u32[]{:S(2)}) collective-permute-start(bf16[384,128]{1,0:T(8,128)(2,1)S(1)} %shard_map.37.after_ref.refs_0_.refs_12_), channel_id=1, source_target_pairs={{0,16},{4,20},{8,24},{12,28},{16,0},{20,4},{24,8},{28,12},{1,17},{... | collective-permute-start | bytes 294920 | tf_op jit(solution)/shard_map/ppermute | solution.py:317
  60.8 1.6 %collective-permute-start.20 = (bf16[384,128]{1,0:T(8,128)(2,1)S(1)}, bf16[384,128]{1,0:T(8,128)(2,1)S(1)}, u32[]{:S(2)}, u32[]{:S(2)}) collective-permute-start(bf16[384,128]{1,0:T(8,128)(2,1)S(1)} %get-tuple-element.57.after_ref.refs_0_), channel_id=1, source_target_pairs={{0,8},{4,12},{8,0},{12,4},{16,24},{20,28},{24,16},{28,20},{1,9},{5... | collective-permute-start | bytes 294920 | tf_op jit(solution)/shard_map/ppermute | solution.py:317
  62.8 1.7 %collective-permute-start.26 = (bf16[384,128]{1,0:T(8,128)(2,1)S(1)}, bf16[384,128]{1,0:T(8,128)(2,1)S(1)}, u32[]{:S(2)}, u32[]{:S(2)}) collective-permute-start(bf16[384,128]{1,0:T(8,128)(2,1)S(1)} %shard_map.37.after_ref.refs_0_.refs_12_), channel_id=1, source_target_pairs={{0,8},{4,12},{8,0},{12,4},{16,24},{20,28},{24,16},{28,20},{1,9},{5... | collective-permute-start | bytes 294920 | tf_op jit(solution)/shard_map/ppermute | solution.py:317
  64.7 1.3 %collective-permute-start.28 = (bf16[384,128]{1,0:T(8,128)(2,1)S(1)}, bf16[384,128]{1,0:T(8,128)(2,1)S(1)}, u32[]{:S(2)}, u32[]{:S(2)}) collective-permute-start(bf16[384,128]{1,0:T(8,128)(2,1)S(1)} %collective-permute-done.27.refs_2_), channel_id=1, source_target_pairs={{0,8},{4,12},{8,0},{12,4},{16,24},{20,28},{24,16},{28,20},{1,9},{5... | collective-permute-start | bytes 294920 | tf_op jit(solution)/shard_map/ppermute | solution.py:317
  66.7 2.1 %collective-permute-done.22.refs_3_ = bf16[384,128]{1,0:T(8,128)(2,1)S(1)} collective-permute-done((bf16[384,128]{1,0:T(8,128)(2,1)S(1)}, bf16[384,128]{1,0:T(8,128)(2,1)S(1)}, u32[]{:S(2)}, u32[]{:S(2)}) %collective-permute-start.22) | collective-permute-done | bytes 98336 | tf_op jit(solution)/shard_map/ppermute | solution.py:317
  68.8 1.0 collective-permute-start.23
  69.8 1.3 %collective-permute-start.24 = (bf16[384,128]{1,0:T(8,128)(2,1)S(1)}, bf16[384,128]{1,0:T(8,128)(2,1)S(1)}, u32[]{:S(2)}, u32[]{:S(2)}) collective-permute-start(bf16[384,128]{1,0:T(8,128)(2,1)S(1)} %get-tuple-element.63), channel_id=1, source_target_pairs={{0,2},{1,3},{2,0},{3,1},{4,6},{5,7},{6,4},{7,5},{8,10},{9,11},{10,... | collective-permute-start | bytes 294920 | tf_op jit(solution)/shard_map/ppermute | solution.py:313
  71.1 1.3 %collective-permute-start.25 = (bf16[384,128]{1,0:T(8,128)(2,1)S(1)}, bf16[384,128]{1,0:T(8,128)(2,1)S(1)}, u32[]{:S(2)}, u32[]{:S(2)}) collective-permute-start(bf16[384,128]{1,0:T(8,128)(2,1)S(1)} %get-tuple-element.64), channel_id=1, source_target_pairs={{0,3},{1,2},{2,1},{3,0},{4,7},{5,6},{6,5},{7,4},{8,11},{9,10},{10,... | collective-permute-start | bytes 294920 | tf_op jit(solution)/shard_map/ppermute | solution.py:313
  72.7 1.0 collective-permute-start.30
  73.6 1.3 %collective-permute-start.31 = (bf16[384,128]{1,0:T(8,128)(2,1)S(1)}, bf16[384,128]{1,0:T(8,128)(2,1)S(1)}, u32[]{:S(2)}, u32[]{:S(2)}) collective-permute-start(bf16[384,128]{1,0:T(8,128)(2,1)S(1)} %get-tuple-element.67), channel_id=1, source_target_pairs={{0,2},{1,3},{2,0},{3,1},{4,6},{5,7},{6,4},{7,5},{8,10},{9,11},{10,... | collective-permute-start | bytes 294920 | tf_op jit(solution)/shard_map/ppermute | solution.py:313
  74.9 1.3 %collective-permute-start.32 = (bf16[384,128]{1,0:T(8,128)(2,1)S(1)}, bf16[384,128]{1,0:T(8,128)(2,1)S(1)}, u32[]{:S(2)}, u32[]{:S(2)}) collective-permute-start(bf16[384,128]{1,0:T(8,128)(2,1)S(1)} %get-tuple-element.68), channel_id=1, source_target_pairs={{0,3},{1,2},{2,1},{3,0},{4,7},{5,6},{6,5},{7,4},{8,11},{9,10},{10,... | collective-permute-start | bytes 294920 | tf_op jit(solution)/shard_map/ppermute | solution.py:313
  76.2 1.0 collective-permute-done.25.refs_3_
  78.7 1.7 %collective-permute-done.32.refs_3_ = bf16[384,128]{1,0:T(8,128)(2,1)S(1)} collective-permute-done((bf16[384,128]{1,0:T(8,128)(2,1)S(1)}, bf16[384,128]{1,0:T(8,128)(2,1)S(1)}, u32[]{:S(2)}, u32[]{:S(2)}) %collective-permute-start.32) | collective-permute-done | bytes 98336 | tf_op jit(solution)/shard_map/ppermute | solution.py:313
  80.6 1.3 %collective-permute-start.36 = (bf16[512,128]{1,0:T(8,128)(2,1)S(1)}, bf16[512,128]{1,0:T(8,128)(2,1)S(1)}, u32[]{:S(2)}, u32[]{:S(2)}) collective-permute-start(bf16[512,128]{1,0:T(8,128)(2,1)S(1)} %get-tuple-element.70.refs_8_), channel_id=1, source_target_pairs={{0,3},{1,2},{2,1},{3,0},{4,7},{5,6},{6,5},{7,4},{8,11},{9,10},{10,... | collective-permute-start | bytes 393224 | tf_op jit(solution)/shard_map/ppermute | solution.py:313
  82.8 1.3 %collective-permute-start.34 = (bf16[512,128]{1,0:T(8,128)(2,1)S(1)}, bf16[512,128]{1,0:T(8,128)(2,1)S(1)}, u32[]{:S(2)}, u32[]{:S(2)}) collective-permute-start(bf16[512,128]{1,0:T(8,128)(2,1)S(1)} %get-tuple-element.70.refs_8_), channel_id=1, source_target_pairs={{0,1},{1,0},{2,3},{3,2},{4,5},{5,4},{6,7},{7,6},{8,9},{9,8},{10,11... | collective-permute-start | bytes 393224 | tf_op jit(solution)/shard_map/ppermute | solution.py:313
  84.1 1.3 %collective-permute-start.39 = (bf16[384,128]{1,0:T(8,128)(2,1)S(1)}, bf16[384,128]{1,0:T(8,128)(2,1)S(1)}, u32[]{:S(2)}, u32[]{:S(2)}) collective-permute-start(bf16[384,128]{1,0:T(8,128)(2,1)S(1)} %shard_map.37.after_ref.refs_0_.refs_12_), channel_id=1, source_target_pairs={{0,3},{1,2},{2,1},{3,0},{4,7},{5,6},{6,5},{7,4},{8,11},{9,10},{10,... | collective-permute-start | bytes 294920 | tf_op jit(solution)/shard_map/ppermute | solution.py:313
  88.7 2.1 %collective-permute-done.35.refs_10_ = bf16[512,128]{1,0:T(8,128)(2,1)S(1)} collective-permute-done((bf16[512,128]{1,0:T(8,128)(2,1)S(1)}, bf16[512,128]{1,0:T(8,128)(2,1)S(1)}, u32[]{:S(2)}, u32[]{:S(2)}) %collective-permute-start.35) | collective-permute-done | bytes 131104 | tf_op jit(solution)/shard_map/ppermute | solution.py:313
  90.8 1.3 %collective-permute-start.42 = (bf16[3,128,128]{2,1,0:T(8,128)(2,1)S(1)}, bf16[3,128,128]{2,1,0:T(8,128)(2,1)S(1)}, u32[]{:S(2)}, u32[]{:S(2)}) collective-permute-start(bf16[3,128,128]{2,1,0:T(8,128)(2,1)S(1)} %get-tuple-element.74), channel_id=1, source_target_pairs={{0,3},{1,2},{2,1},{3,0},{4,7},{5,6},{6,5},{7,4},{8,11},{9,10},{10,... | collective-permute-start | bytes 294920 | tf_op jit(solution)/shard_map/ppermute | solution.py:313
  93.0 1.3 %collective-permute-start.40 = (bf16[3,128,128]{2,1,0:T(8,128)(2,1)S(1)}, bf16[3,128,128]{2,1,0:T(8,128)(2,1)S(1)}, u32[]{:S(2)}, u32[]{:S(2)}) collective-permute-start(bf16[3,128,128]{2,1,0:T(8,128)(2,1)S(1)} %get-tuple-element.74), channel_id=1, source_target_pairs={{0,1},{1,0},{2,3},{3,2},{4,5},{5,4},{6,7},{7,6},{8,9},{9,8},{10,11... | collective-permute-start | bytes 294920 | tf_op jit(solution)/shard_map/ppermute | solution.py:313
  94.8 1.2 %shard_map.43 = (bf16[1536,512]{1,0:T(8,128)(2,1)S(1)}, bf16[1536,512]{1,0:T(8,128)(2,1)S(1)}, bf16[1536,256]{1,0:T(8,128)(2,1)S(1)}, f32[1536,256]{1,0:T(8,128)S(1)}, f32[128,128]{1,0:T(8,128)S(1)}) custom-call(f32[3,128,128]{2,1,0:T(8,128)S(1)} %get-tuple-element.69.after_ref.own, bf16[2,1536,128]{2,1,0:T(8,128)(2,1)S(1)} %copy-done.1, ...), custom_call_target="tpu_custom_call" | custom-call | tf_op jit(solution)/shard_map/pallas_call | solution.py:52
  96.0 1.4 %collective-permute-done.42.refs_2_ = bf16[3,128,128]{2,1,0:T(8,128)(2,1)S(1)} collective-permute-done((bf16[3,128,128]{2,1,0:T(8,128)(2,1)S(1)}, bf16[3,128,128]{2,1,0:T(8,128)(2,1)S(1)}, u32[]{:S(2)}, u32[]{:S(2)}) %collective-permute-start.42) | collective-permute-done | bytes 98336 | tf_op jit(solution)/shard_map/ppermute | solution.py:313
  97.4 1.2 %collective-permute-done.41.refs_1_ = bf16[3,128,128]{2,1,0:T(8,128)(2,1)S(1)} collective-permute-done((bf16[3,128,128]{2,1,0:T(8,128)(2,1)S(1)}, bf16[3,128,128]{2,1,0:T(8,128)(2,1)S(1)}, u32[]{:S(2)}, u32[]{:S(2)}) %collective-permute-start.41) | collective-permute-done | bytes 98336 | tf_op jit(solution)/shard_map/ppermute | solution.py:313
  98.6 9.7 %update.1 = bf16[1536,3072]{1,0:T(8,128)(2,1)} custom-call(bf16[1536,3072]{1,0:T(8,128)(2,1)S(1)} %load.1.refs_4_.a_ref, bf16[2,1536,128]{2,1,0:T(8,128)(2,1)S(1)} %copy-done.1, bf16[1536,256]{1,0:T(8,128)(2,1)S(1)} %get-tuple-element.71.x_ref, f32[1536,256]{1,0:T(8,128)S(1)} %get-tuple-element.72.y_ref, f32[128,128]{1,0:T(8,128)S(1)} %get-tuple-element.73.s_ref, ...), custom_call_target="tpu_custom_call" | custom-call | tf_op jit(solution)/shard_map/update/pallas_call | solution.py:294
  (60 shorter events, 12.8 us)
Async XLA Ops:
  0.0 1.1 %copy-start = (bf16[2,1536,128]{2,1,0:T(8,128)(2,1)S(1)}, bf16[2,1536,128]{2,1,0:T(8,128)(2,1)}, u32[]{:S(2)}) copy-start(bf16[2,1536,128]{2,1,0:T(8,128)(2,1)} %panels_ref.5) | copy-start | bytes 2359300
  1.2 8.9 %collective-permute-start = (bf16[384,128]{1,0:T(8,128)(2,1)S(1)}, bf16[384,128]{1,0:T(8,128)(2,1)S(1)}, u32[]{:S(2)}, u32[]{:S(2)}) collective-permute-start(bf16[384,128]{1,0:T(8,128)(2,1)S(1)} %get-tuple-element.41.refs_0_), channel_id=1, source_target_pairs={{0,16},{4,20},{8,24},{12,28},{16,0},{20,4},{24,8},{28,12},{1,17},{... | collective-permute-start | bytes 294920 | tf_op jit(solution)/shard_map/ppermute | solution.py:317
  5.3 5.6 %collective-permute-start.1 = (bf16[384,128]{1,0:T(8,128)(2,1)S(1)}, bf16[384,128]{1,0:T(8,128)(2,1)S(1)}, u32[]{:S(2)}, u32[]{:S(2)}) collective-permute-start(bf16[384,128]{1,0:T(8,128)(2,1)S(1)} %get-tuple-element.41.refs_0_), channel_id=1, source_target_pairs={{0,8},{4,12},{8,0},{12,4},{16,24},{20,28},{24,16},{28,20},{1,9},{5... | collective-permute-start | bytes 294920 | tf_op jit(solution)/shard_map/ppermute | solution.py:317
  10.1 4.6 %collective-permute-start.2 = (bf16[384,128]{1,0:T(8,128)(2,1)S(1)}, bf16[384,128]{1,0:T(8,128)(2,1)S(1)}, u32[]{:S(2)}, u32[]{:S(2)}) collective-permute-start(bf16[384,128]{1,0:T(8,128)(2,1)S(1)} %collective-permute-done.refs_0_.refs_2_), channel_id=1, source_target_pairs={{0,8},{4,12},{8,0},{12,4},{16,24},{20,28},{24,16},{28,20},{1,9},{5... | collective-permute-start | bytes 294920 | tf_op jit(solution)/shard_map/ppermute | solution.py:317
  14.8 7.3 %collective-permute-start.3 = (bf16[384,128]{1,0:T(8,128)(2,1)S(1)}, bf16[384,128]{1,0:T(8,128)(2,1)S(1)}, u32[]{:S(2)}, u32[]{:S(2)}) collective-permute-start(bf16[384,128]{1,0:T(8,128)(2,1)S(1)} %get-tuple-element.44), channel_id=1, source_target_pairs={{0,1},{1,0},{2,3},{3,2},{4,5},{5,4},{6,7},{7,6},{8,9},{9,8},{10,11... | collective-permute-start | bytes 294920 | tf_op jit(solution)/shard_map/ppermute | solution.py:313
  16.6 5.5 %collective-permute-start.4 = (bf16[384,128]{1,0:T(8,128)(2,1)S(1)}, bf16[384,128]{1,0:T(8,128)(2,1)S(1)}, u32[]{:S(2)}, u32[]{:S(2)}) collective-permute-start(bf16[384,128]{1,0:T(8,128)(2,1)S(1)} %get-tuple-element.45), channel_id=1, source_target_pairs={{0,2},{1,3},{2,0},{3,1},{4,6},{5,7},{6,4},{7,5},{8,10},{9,11},{10,... | collective-permute-start | bytes 294920 | tf_op jit(solution)/shard_map/ppermute | solution.py:313
  18.1 5.5 %collective-permute-start.5 = (bf16[384,128]{1,0:T(8,128)(2,1)S(1)}, bf16[384,128]{1,0:T(8,128)(2,1)S(1)}, u32[]{:S(2)}, u32[]{:S(2)}) collective-permute-start(bf16[384,128]{1,0:T(8,128)(2,1)S(1)} %get-tuple-element.46), channel_id=1, source_target_pairs={{0,3},{1,2},{2,1},{3,0},{4,7},{5,6},{6,5},{7,4},{8,11},{9,10},{10,... | collective-permute-start | bytes 294920 | tf_op jit(solution)/shard_map/ppermute | solution.py:313
  23.6 16.6 %collective-permute-start.6 = (bf16[1536,128]{1,0:T(8,128)(2,1)S(1)}, bf16[1536,128]{1,0:T(8,128)(2,1)S(1)}, u32[]{:S(2)}, u32[]{:S(2)}) collective-permute-start(bf16[1536,128]{1,0:T(8,128)(2,1)S(1)} %shard_map.31.after_ref.refs_0_.refs_2_.refs_4_), channel_id=1, source_target_pairs={{0,4},{4,0},{8,12},{12,8},{16,20},{20,16},{24,28},{28,24},{1,5},{5... | collective-permute-start | bytes 1179656 | tf_op jit(solution)/shard_map/ppermute | solution.py:323
  23.7 8.3 %collective-permute-start.8 = (bf16[384,128]{1,0:T(8,128)(2,1)S(1)}, bf16[384,128]{1,0:T(8,128)(2,1)S(1)}, u32[]{:S(2)}, u32[]{:S(2)}) collective-permute-start(bf16[384,128]{1,0:T(8,128)(2,1)S(1)} %shard_map.29.after_ref.refs_0_), channel_id=1, source_target_pairs={{0,16},{4,20},{8,24},{12,28},{16,0},{20,4},{24,8},{28,12},{1,17},{... | collective-permute-start | bytes 294920 | tf_op jit(solution)/shard_map/ppermute | solution.py:317
  26.1 6.2 %collective-permute-start.7 = (bf16[384,128]{1,0:T(8,128)(2,1)S(1)}, bf16[384,128]{1,0:T(8,128)(2,1)S(1)}, u32[]{:S(2)}, u32[]{:S(2)}) collective-permute-start(bf16[384,128]{1,0:T(8,128)(2,1)S(1)} %shard_map.29.after_ref.refs_0_), channel_id=1, source_target_pairs={{0,8},{4,12},{8,0},{12,4},{16,24},{20,28},{24,16},{28,20},{1,9},{5... | collective-permute-start | bytes 294920 | tf_op jit(solution)/shard_map/ppermute | solution.py:317
  32.0 4.6 %collective-permute-start.9 = (bf16[384,128]{1,0:T(8,128)(2,1)S(1)}, bf16[384,128]{1,0:T(8,128)(2,1)S(1)}, u32[]{:S(2)}, u32[]{:S(2)}) collective-permute-start(bf16[384,128]{1,0:T(8,128)(2,1)S(1)} %collective-permute-done.8.refs_2_), channel_id=1, source_target_pairs={{0,8},{4,12},{8,0},{12,4},{16,24},{20,28},{24,16},{28,20},{1,9},{5... | collective-permute-start | bytes 294920 | tf_op jit(solution)/shard_map/ppermute | solution.py:317
  36.7 6.2 %collective-permute-start.10 = (bf16[384,128]{1,0:T(8,128)(2,1)S(1)}, bf16[384,128]{1,0:T(8,128)(2,1)S(1)}, u32[]{:S(2)}, u32[]{:S(2)}) collective-permute-start(bf16[384,128]{1,0:T(8,128)(2,1)S(1)} %get-tuple-element.48), channel_id=1, source_target_pairs={{0,1},{1,0},{2,3},{3,2},{4,5},{5,4},{6,7},{7,6},{8,9},{9,8},{10,11... | collective-permute-start | bytes 294920 | tf_op jit(solution)/shard_map/ppermute | solution.py:313
  37.3 5.6 %collective-permute-start.11 = (bf16[384,128]{1,0:T(8,128)(2,1)S(1)}, bf16[384,128]{1,0:T(8,128)(2,1)S(1)}, u32[]{:S(2)}, u32[]{:S(2)}) collective-permute-start(bf16[384,128]{1,0:T(8,128)(2,1)S(1)} %get-tuple-element.49), channel_id=1, source_target_pairs={{0,2},{1,3},{2,0},{3,1},{4,6},{5,7},{6,4},{7,5},{8,10},{9,11},{10,... | collective-permute-start | bytes 294920 | tf_op jit(solution)/shard_map/ppermute | solution.py:313
  38.5 5.5 %collective-permute-start.12 = (bf16[384,128]{1,0:T(8,128)(2,1)S(1)}, bf16[384,128]{1,0:T(8,128)(2,1)S(1)}, u32[]{:S(2)}, u32[]{:S(2)}) collective-permute-start(bf16[384,128]{1,0:T(8,128)(2,1)S(1)} %get-tuple-element.50), channel_id=1, source_target_pairs={{0,3},{1,2},{2,1},{3,0},{4,7},{5,6},{6,5},{7,4},{8,11},{9,10},{10,... | collective-permute-start | bytes 294920 | tf_op jit(solution)/shard_map/ppermute | solution.py:313
  44.0 3.6 %collective-permute-start.13 = (bf16[1536,128]{1,0:T(8,128)(2,1)S(1)}, bf16[1536,128]{1,0:T(8,128)(2,1)S(1)}, u32[]{:S(2)}, u32[]{:S(2)}) collective-permute-start(bf16[1536,128]{1,0:T(8,128)(2,1)S(1)} %shard_map.34.after_ref.refs_0_.refs_2_.refs_6_), channel_id=1, source_target_pairs={{0,4},{4,0},{8,12},{12,8},{16,20},{20,16},{24,28},{28,24},{1,5},{5... | collective-permute-start | bytes 1179656 | tf_op jit(solution)/shard_map/ppermute | solution.py:323
  44.1 8.8 %collective-permute-start.14 = (bf16[384,128]{1,0:T(8,128)(2,1)S(1)}, bf16[384,128]{1,0:T(8,128)(2,1)S(1)}, u32[]{:S(2)}, u32[]{:S(2)}) collective-permute-start(bf16[384,128]{1,0:T(8,128)(2,1)S(1)} %get-tuple-element.53), channel_id=1, source_target_pairs={{0,1},{1,0},{2,3},{3,2},{4,5},{5,4},{6,7},{7,6},{8,9},{9,8},{10,11... | collective-permute-start | bytes 294920 | tf_op jit(solution)/shard_map/ppermute | solution.py:313
  45.0 9.0 %collective-permute-start.15 = (bf16[384,128]{1,0:T(8,128)(2,1)S(1)}, bf16[384,128]{1,0:T(8,128)(2,1)S(1)}, u32[]{:S(2)}, u32[]{:S(2)}) collective-permute-start(bf16[384,128]{1,0:T(8,128)(2,1)S(1)} %get-tuple-element.54), channel_id=1, source_target_pairs={{0,2},{1,3},{2,0},{3,1},{4,6},{5,7},{6,4},{7,5},{8,10},{9,11},{10,... | collective-permute-start | bytes 294920 | tf_op jit(solution)/shard_map/ppermute | solution.py:313
  46.5 48.3 %copy-start.1 = (bf16[2,1536,128]{2,1,0:T(8,128)(2,1)S(1)}, bf16[2,1536,128]{2,1,0:T(8,128)(2,1)}, u32[]{:S(2)}) copy-start(bf16[2,1536,128]{2,1,0:T(8,128)(2,1)} %panels_ref.5) | copy-start | bytes 2359300
  46.5 7.5 %collective-permute-start.16 = (bf16[384,128]{1,0:T(8,128)(2,1)S(1)}, bf16[384,128]{1,0:T(8,128)(2,1)S(1)}, u32[]{:S(2)}, u32[]{:S(2)}) collective-permute-start(bf16[384,128]{1,0:T(8,128)(2,1)S(1)} %get-tuple-element.55), channel_id=1, source_target_pairs={{0,3},{1,2},{2,1},{3,0},{4,7},{5,6},{6,5},{7,4},{8,11},{9,10},{10,... | collective-permute-start | bytes 294920 | tf_op jit(solution)/shard_map/ppermute | solution.py:313
  50.5 5.8 %collective-permute-start.17 = (bf16[384,128]{1,0:T(8,128)(2,1)S(1)}, bf16[384,128]{1,0:T(8,128)(2,1)S(1)}, u32[]{:S(2)}, u32[]{:S(2)}) collective-permute-start(bf16[384,128]{1,0:T(8,128)(2,1)S(1)} %get-tuple-element.58), channel_id=1, source_target_pairs={{0,1},{1,0},{2,3},{3,2},{4,5},{5,4},{6,7},{7,6},{8,9},{9,8},{10,11... | collective-permute-start | bytes 294920 | tf_op jit(solution)/shard_map/ppermute | solution.py:313
  51.4 5.7 %collective-permute-start.18 = (bf16[384,128]{1,0:T(8,128)(2,1)S(1)}, bf16[384,128]{1,0:T(8,128)(2,1)S(1)}, u32[]{:S(2)}, u32[]{:S(2)}) collective-permute-start(bf16[384,128]{1,0:T(8,128)(2,1)S(1)} %get-tuple-element.59), channel_id=1, source_target_pairs={{0,2},{1,3},{2,0},{3,1},{4,6},{5,7},{6,4},{7,5},{8,10},{9,11},{10,... | collective-permute-start | bytes 294920 | tf_op jit(solution)/shard_map/ppermute | solution.py:313
  52.9 5.5 %collective-permute-start.19 = (bf16[384,128]{1,0:T(8,128)(2,1)S(1)}, bf16[384,128]{1,0:T(8,128)(2,1)S(1)}, u32[]{:S(2)}, u32[]{:S(2)}) collective-permute-start(bf16[384,128]{1,0:T(8,128)(2,1)S(1)} %get-tuple-element.60), channel_id=1, source_target_pairs={{0,3},{1,2},{2,1},{3,0},{4,7},{5,6},{6,5},{7,4},{8,11},{9,10},{10,... | collective-permute-start | bytes 294920 | tf_op jit(solution)/shard_map/ppermute | solution.py:313
  54.1 8.4 %collective-permute-start.21 = (bf16[384,128]{1,0:T(8,128)(2,1)S(1)}, bf16[384,128]{1,0:T(8,128)(2,1)S(1)}, u32[]{:S(2)}, u32[]{:S(2)}) collective-permute-start(bf16[384,128]{1,0:T(8,128)(2,1)S(1)} %get-tuple-element.57.after_ref.refs_0_), channel_id=1, source_target_pairs={{0,16},{4,20},{8,24},{12,28},{16,0},{20,4},{24,8},{28,12},{1,17},{... | collective-permute-start | bytes 294920 | tf_op jit(solution)/shard_map/ppermute | solution.py:317
  58.5 6.3 %collective-permute-start.27 = (bf16[384,128]{1,0:T(8,128)(2,1)S(1)}, bf16[384,128]{1,0:T(8,128)(2,1)S(1)}, u32[]{:S(2)}, u32[]{:S(2)}) collective-permute-start(bf16[384,128]{1,0:T(8,128)(2,1)S(1)} %shard_map.37.after_ref.refs_0_.refs_12_), channel_id=1, source_target_pairs={{0,16},{4,20},{8,24},{12,28},{16,0},{20,4},{24,8},{28,12},{1,17},{... | collective-permute-start | bytes 294920 | tf_op jit(solution)/shard_map/ppermute | solution.py:317
  60.8 5.9 %collective-permute-start.20 = (bf16[384,128]{1,0:T(8,128)(2,1)S(1)}, bf16[384,128]{1,0:T(8,128)(2,1)S(1)}, u32[]{:S(2)}, u32[]{:S(2)}) collective-permute-start(bf16[384,128]{1,0:T(8,128)(2,1)S(1)} %get-tuple-element.57.after_ref.refs_0_), channel_id=1, source_target_pairs={{0,8},{4,12},{8,0},{12,4},{16,24},{20,28},{24,16},{28,20},{1,9},{5... | collective-permute-start | bytes 294920 | tf_op jit(solution)/shard_map/ppermute | solution.py:317
  62.5 6.3 %collective-permute-start.22 = (bf16[384,128]{1,0:T(8,128)(2,1)S(1)}, bf16[384,128]{1,0:T(8,128)(2,1)S(1)}, u32[]{:S(2)}, u32[]{:S(2)}) collective-permute-start(bf16[384,128]{1,0:T(8,128)(2,1)S(1)} %collective-permute-done.21.refs_2_), channel_id=1, source_target_pairs={{0,8},{4,12},{8,0},{12,4},{16,24},{20,28},{24,16},{28,20},{1,9},{5... | collective-permute-start | bytes 294920 | tf_op jit(solution)/shard_map/ppermute | solution.py:317
  62.8 9.6 %collective-permute-start.26 = (bf16[384,128]{1,0:T(8,128)(2,1)S(1)}, bf16[384,128]{1,0:T(8,128)(2,1)S(1)}, u32[]{:S(2)}, u32[]{:S(2)}) collective-permute-start(bf16[384,128]{1,0:T(8,128)(2,1)S(1)} %shard_map.37.after_ref.refs_0_.refs_12_), channel_id=1, source_target_pairs={{0,8},{4,12},{8,0},{12,4},{16,24},{20,28},{24,16},{28,20},{1,9},{5... | collective-permute-start | bytes 294920 | tf_op jit(solution)/shard_map/ppermute | solution.py:317
  64.7 7.7 %collective-permute-start.28 = (bf16[384,128]{1,0:T(8,128)(2,1)S(1)}, bf16[384,128]{1,0:T(8,128)(2,1)S(1)}, u32[]{:S(2)}, u32[]{:S(2)}) collective-permute-start(bf16[384,128]{1,0:T(8,128)(2,1)S(1)} %collective-permute-done.27.refs_2_), channel_id=1, source_target_pairs={{0,8},{4,12},{8,0},{12,4},{16,24},{20,28},{24,16},{28,20},{1,9},{5... | collective-permute-start | bytes 294920 | tf_op jit(solution)/shard_map/ppermute | solution.py:317
  68.8 6.1 %collective-permute-start.23 = (bf16[384,128]{1,0:T(8,128)(2,1)S(1)}, bf16[384,128]{1,0:T(8,128)(2,1)S(1)}, u32[]{:S(2)}, u32[]{:S(2)}) collective-permute-start(bf16[384,128]{1,0:T(8,128)(2,1)S(1)} %get-tuple-element.62), channel_id=1, source_target_pairs={{0,1},{1,0},{2,3},{3,2},{4,5},{5,4},{6,7},{7,6},{8,9},{9,8},{10,11... | collective-permute-start | bytes 294920 | tf_op jit(solution)/shard_map/ppermute | solution.py:313
  69.8 6.4 %collective-permute-start.24 = (bf16[384,128]{1,0:T(8,128)(2,1)S(1)}, bf16[384,128]{1,0:T(8,128)(2,1)S(1)}, u32[]{:S(2)}, u32[]{:S(2)}) collective-permute-start(bf16[384,128]{1,0:T(8,128)(2,1)S(1)} %get-tuple-element.63), channel_id=1, source_target_pairs={{0,2},{1,3},{2,0},{3,1},{4,6},{5,7},{6,4},{7,5},{8,10},{9,11},{10,... | collective-permute-start | bytes 294920 | tf_op jit(solution)/shard_map/ppermute | solution.py:313
  71.1 6.1 %collective-permute-start.25 = (bf16[384,128]{1,0:T(8,128)(2,1)S(1)}, bf16[384,128]{1,0:T(8,128)(2,1)S(1)}, u32[]{:S(2)}, u32[]{:S(2)}) collective-permute-start(bf16[384,128]{1,0:T(8,128)(2,1)S(1)} %get-tuple-element.64), channel_id=1, source_target_pairs={{0,3},{1,2},{2,1},{3,0},{4,7},{5,6},{6,5},{7,4},{8,11},{9,10},{10,... | collective-permute-start | bytes 294920 | tf_op jit(solution)/shard_map/ppermute | solution.py:313
  72.7 5.4 %collective-permute-start.30 = (bf16[384,128]{1,0:T(8,128)(2,1)S(1)}, bf16[384,128]{1,0:T(8,128)(2,1)S(1)}, u32[]{:S(2)}, u32[]{:S(2)}) collective-permute-start(bf16[384,128]{1,0:T(8,128)(2,1)S(1)} %get-tuple-element.66), channel_id=1, source_target_pairs={{0,1},{1,0},{2,3},{3,2},{4,5},{5,4},{6,7},{7,6},{8,9},{9,8},{10,11... | collective-permute-start | bytes 294920 | tf_op jit(solution)/shard_map/ppermute | solution.py:313
  73.6 5.1 %collective-permute-start.31 = (bf16[384,128]{1,0:T(8,128)(2,1)S(1)}, bf16[384,128]{1,0:T(8,128)(2,1)S(1)}, u32[]{:S(2)}, u32[]{:S(2)}) collective-permute-start(bf16[384,128]{1,0:T(8,128)(2,1)S(1)} %get-tuple-element.67), channel_id=1, source_target_pairs={{0,2},{1,3},{2,0},{3,1},{4,6},{5,7},{6,4},{7,5},{8,10},{9,11},{10,... | collective-permute-start | bytes 294920 | tf_op jit(solution)/shard_map/ppermute | solution.py:313
  74.9 5.5 %collective-permute-start.32 = (bf16[384,128]{1,0:T(8,128)(2,1)S(1)}, bf16[384,128]{1,0:T(8,128)(2,1)S(1)}, u32[]{:S(2)}, u32[]{:S(2)}) collective-permute-start(bf16[384,128]{1,0:T(8,128)(2,1)S(1)} %get-tuple-element.68), channel_id=1, source_target_pairs={{0,3},{1,2},{2,1},{3,0},{4,7},{5,6},{6,5},{7,4},{8,11},{9,10},{10,... | collective-permute-start | bytes 294920 | tf_op jit(solution)/shard_map/ppermute | solution.py:313
  77.2 6.9 %collective-permute-start.29 = (bf16[1536,128]{1,0:T(8,128)(2,1)S(1)}, bf16[1536,128]{1,0:T(8,128)(2,1)S(1)}, u32[]{:S(2)}, u32[]{:S(2)}) collective-permute-start(bf16[1536,128]{1,0:T(8,128)(2,1)S(1)} %shard_map.40.refs_4_.refs_0_), channel_id=1, source_target_pairs={{0,4},{4,0},{8,12},{12,8},{16,20},{20,16},{24,28},{28,24},{1,5},{5... | collective-permute-start | bytes 1179656 | tf_op jit(solution)/shard_map/ppermute | solution.py:323
  80.5 4.9 %collective-permute-start.33 = (bf16[1536,128]{1,0:T(8,128)(2,1)S(1)}, bf16[1536,128]{1,0:T(8,128)(2,1)S(1)}, u32[]{:S(2)}, u32[]{:S(2)}) collective-permute-start(bf16[1536,128]{1,0:T(8,128)(2,1)S(1)} %shard_map.41.refs_6_.refs_2_), channel_id=1, source_target_pairs={{0,4},{4,0},{8,12},{12,8},{16,20},{20,16},{24,28},{28,24},{1,5},{5... | collective-permute-start | bytes 1179656 | tf_op jit(solution)/shard_map/ppermute | solution.py:323
  80.6 7.4 %collective-permute-start.36 = (bf16[512,128]{1,0:T(8,128)(2,1)S(1)}, bf16[512,128]{1,0:T(8,128)(2,1)S(1)}, u32[]{:S(2)}, u32[]{:S(2)}) collective-permute-start(bf16[512,128]{1,0:T(8,128)(2,1)S(1)} %get-tuple-element.70.refs_8_), channel_id=1, source_target_pairs={{0,3},{1,2},{2,1},{3,0},{4,7},{5,6},{6,5},{7,4},{8,11},{9,10},{10,... | collective-permute-start | bytes 393224 | tf_op jit(solution)/shard_map/ppermute | solution.py:313
  81.9 8.9 %collective-permute-start.35 = (bf16[512,128]{1,0:T(8,128)(2,1)S(1)}, bf16[512,128]{1,0:T(8,128)(2,1)S(1)}, u32[]{:S(2)}, u32[]{:S(2)}) collective-permute-start(bf16[512,128]{1,0:T(8,128)(2,1)S(1)} %get-tuple-element.70.refs_8_), channel_id=1, source_target_pairs={{0,2},{1,3},{2,0},{3,1},{4,6},{5,7},{6,4},{7,5},{8,10},{9,11},{10,... | collective-permute-start | bytes 393224 | tf_op jit(solution)/shard_map/ppermute | solution.py:313
  82.8 9.3 %collective-permute-start.34 = (bf16[512,128]{1,0:T(8,128)(2,1)S(1)}, bf16[512,128]{1,0:T(8,128)(2,1)S(1)}, u32[]{:S(2)}, u32[]{:S(2)}) collective-permute-start(bf16[512,128]{1,0:T(8,128)(2,1)S(1)} %get-tuple-element.70.refs_8_), channel_id=1, source_target_pairs={{0,1},{1,0},{2,3},{3,2},{4,5},{5,4},{6,7},{7,6},{8,9},{9,8},{10,11... | collective-permute-start | bytes 393224 | tf_op jit(solution)/shard_map/ppermute | solution.py:313
  84.1 8.9 %collective-permute-start.39 = (bf16[384,128]{1,0:T(8,128)(2,1)S(1)}, bf16[384,128]{1,0:T(8,128)(2,1)S(1)}, u32[]{:S(2)}, u32[]{:S(2)}) collective-permute-start(bf16[384,128]{1,0:T(8,128)(2,1)S(1)} %shard_map.37.after_ref.refs_0_.refs_12_), channel_id=1, source_target_pairs={{0,3},{1,2},{2,1},{3,0},{4,7},{5,6},{6,5},{7,4},{8,11},{9,10},{10,... | collective-permute-start | bytes 294920 | tf_op jit(solution)/shard_map/ppermute | solution.py:313
  85.4 9.4 %collective-permute-start.38 = (bf16[384,128]{1,0:T(8,128)(2,1)S(1)}, bf16[384,128]{1,0:T(8,128)(2,1)S(1)}, u32[]{:S(2)}, u32[]{:S(2)}) collective-permute-start(bf16[384,128]{1,0:T(8,128)(2,1)S(1)} %shard_map.37.after_ref.refs_0_.refs_12_), channel_id=1, source_target_pairs={{0,2},{1,3},{2,0},{3,1},{4,6},{5,7},{6,4},{7,5},{8,10},{9,11},{10,... | collective-permute-start | bytes 294920 | tf_op jit(solution)/shard_map/ppermute | solution.py:313
  88.0 6.8 %collective-permute-start.37 = (bf16[384,128]{1,0:T(8,128)(2,1)S(1)}, bf16[384,128]{1,0:T(8,128)(2,1)S(1)}, u32[]{:S(2)}, u32[]{:S(2)}) collective-permute-start(bf16[384,128]{1,0:T(8,128)(2,1)S(1)} %shard_map.37.after_ref.refs_0_.refs_12_), channel_id=1, source_target_pairs={{0,1},{1,0},{2,3},{3,2},{4,5},{5,4},{6,7},{7,6},{8,9},{9,8},{10,11... | collective-permute-start | bytes 294920 | tf_op jit(solution)/shard_map/ppermute | solution.py:313
  90.8 6.6 %collective-permute-start.42 = (bf16[3,128,128]{2,1,0:T(8,128)(2,1)S(1)}, bf16[3,128,128]{2,1,0:T(8,128)(2,1)S(1)}, u32[]{:S(2)}, u32[]{:S(2)}) collective-permute-start(bf16[3,128,128]{2,1,0:T(8,128)(2,1)S(1)} %get-tuple-element.74), channel_id=1, source_target_pairs={{0,3},{1,2},{2,1},{3,0},{4,7},{5,6},{6,5},{7,4},{8,11},{9,10},{10,... | collective-permute-start | bytes 294920 | tf_op jit(solution)/shard_map/ppermute | solution.py:313
  92.1 6.5 %collective-permute-start.41 = (bf16[3,128,128]{2,1,0:T(8,128)(2,1)S(1)}, bf16[3,128,128]{2,1,0:T(8,128)(2,1)S(1)}, u32[]{:S(2)}, u32[]{:S(2)}) collective-permute-start(bf16[3,128,128]{2,1,0:T(8,128)(2,1)S(1)} %get-tuple-element.74), channel_id=1, source_target_pairs={{0,2},{1,3},{2,0},{3,1},{4,6},{5,7},{6,4},{7,5},{8,10},{9,11},{10,... | collective-permute-start | bytes 294920 | tf_op jit(solution)/shard_map/ppermute | solution.py:313
  93.0 5.6 %collective-permute-start.40 = (bf16[3,128,128]{2,1,0:T(8,128)(2,1)S(1)}, bf16[3,128,128]{2,1,0:T(8,128)(2,1)S(1)}, u32[]{:S(2)}, u32[]{:S(2)}) collective-permute-start(bf16[3,128,128]{2,1,0:T(8,128)(2,1)S(1)} %get-tuple-element.74), channel_id=1, source_target_pairs={{0,1},{1,0},{2,3},{3,2},{4,5},{5,4},{6,7},{7,6},{8,9},{9,8},{10,11... | collective-permute-start | bytes 294920 | tf_op jit(solution)/shard_map/ppermute | solution.py:313
